TPU v7x, 768 devices: a whole 4x8x12 slice. The times are simulated.
768 devices in a mesh: az: 16 (over z_lo, x), rad: 48 (over y, z_hi, core).
Axes of the slice: x: 4, y: 8, z: 12 (z_hi: 3, z_lo: 4; z = z_hi * 4 + z_lo), core: 2. Of those that a mesh axis runs over, the one named last changes fastest.
Arguments:
- fields: float32 [5, 2, 384, 2048], P(None, None, 'rad', 'az'), may hold values from -6 to 6
- velocity: float32 [2, 384, 2048], P(None, 'rad', 'az'), may hold values from -0.5 to 0.5
- offsets: int32 [384], P('rad'), may hold values from 0 to 1024, as said below
Outputs:
- fields_out: float32 [5, 2, 384, 2048], P(None, None, 'rad', 'az')
Inputs may be any that keep to these rules, and one draw needn't show every extreme that they name: `offsets`: offsets never rise with the radius; the innermost row has 1024 and the outermost 0.
All inputs are finite; a program needn't handle non-finite values.
Results may differ from a plain program's by a relative error of at most 0.00002.
Values sent between devices are 32-bit elements; how exact they have to be, the bound alone decides.
No kernel may reach another device: no remote copies, remote signals or barrier semaphores. Data moves between devices by JAX's collectives and lax.ppermute only.
A program may use at most 32 MiB of HBM per device.

v0:
```python
import jax
import jax.numpy as jnp
from jax import lax
from jax.sharding import PartitionSpec as P

STEPS = 2


viscosity = 0.05


def with_halo(block, sides, width, periodic):
    for axis, dim in sides:
        count = lax.axis_size(axis)
        forward = [(i, i + 1) for i in range(count - 1)]
        if periodic:
            forward.append((count - 1, 0))
        backward = [(target, source) for source, target in forward]
        low = lax.ppermute(
            lax.slice_in_dim(block, block.shape[dim] - width, None, axis=dim), axis, forward
        )
        high = lax.ppermute(lax.slice_in_dim(block, 0, width, axis=dim), axis, backward)
        block = jnp.concatenate([low, block, high], axis=dim)
    return block


def from_behind(block, axis, distance):
    devices = range(lax.axis_size(axis))
    route = [((i - distance) % len(devices), i) for i in devices]
    return lax.ppermute(block, axis, route)


def stencil(padded, velocity):
    rows = velocity.shape[1]
    cols = velocity.shape[2]
    centre = padded[:, :, 2 : 2 + rows, 2 : 2 + cols]
    r_m2 = padded[:, :, 0:rows, 2 : 2 + cols]
    r_m1 = padded[:, :, 1 : 1 + rows, 2 : 2 + cols]
    r_p1 = padded[:, :, 3 : 3 + rows, 2 : 2 + cols]
    r_p2 = padded[:, :, 4 : 4 + rows, 2 : 2 + cols]
    p_m2 = padded[:, :, 2 : 2 + rows, 0:cols]
    p_m1 = padded[:, :, 2 : 2 + rows, 1 : 1 + cols]
    p_p1 = padded[:, :, 2 : 2 + rows, 3 : 3 + cols]
    p_p2 = padded[:, :, 2 : 2 + rows, 4 : 4 + cols]
    slope_r = (r_m2 - 8.0 * r_m1 + 8.0 * r_p1 - r_p2) / 12.0
    slope_p = (p_m2 - 8.0 * p_m1 + 8.0 * p_p1 - p_p2) / 12.0
    curve_r = (-r_m2 + 16.0 * r_m1 - 30.0 * centre + 16.0 * r_p1 - r_p2) / 12.0
    curve_p = (-p_m2 + 16.0 * p_m1 - 30.0 * centre + 16.0 * p_p1 - p_p2) / 12.0
    return -velocity[1] * slope_p - velocity[0] * slope_r + viscosity * (curve_r + curve_p)


def rim_two(state):
    radial = with_halo(state, (("rad", 2),), 2, False)
    return with_halo(radial, (("az", 3),), 2, True)


def shift_hops(state, offsets):
    columns = state.shape[3]
    cycle_size = lax.axis_size("az")
    whole_hops = offsets // columns
    cell_rest = offsets % columns
    carried = state
    for digit_index in range((cycle_size // 2).bit_length()):
        arrived = from_behind(carried, "az", 1 << digit_index)
        chosen = whole_hops // (1 << digit_index) % 2 == 1
        carried = jnp.where(chosen[None, None, :, None], arrived, carried)
    previous = from_behind(carried, "az", 1)
    window = jnp.concatenate([previous, carried], axis=3)
    for bit_index in range(columns.bit_length()):
        amount = 1 << bit_index
        rolled = jnp.roll(window, amount, axis=3)
        chosen = cell_rest // amount % 2 == 1
        window = jnp.where(chosen[None, None, :, None], rolled, window)
    return window[:, :, :, columns:]


def shards(fields, velocity, offsets):
    state = fields
    for step_index in range(STEPS):
        section_one = state + stencil(rim_two(state), velocity)
        state = 0.5 * (state + section_one + stencil(rim_two(section_one), velocity))
        state = shift_hops(state, offsets)
    return state


def solution(mesh):
    placed = (P(None, None, "rad", "az"), P(None, "rad", "az"), P("rad"))
    return jax.shard_map(
        shards, mesh=mesh, in_specs=placed, out_specs=P(None, None, "rad", "az"), check_vma=False
    )
```

profile of v0, /device:TPU:32, one launch (start us, length us, event | category | flops | bytes accessed | tf_op | source)
XLA Modules:
  0.0 199.6 jit_solution(3192692730584286144)
XLA Ops:
  0.0 0.9 fusion.49
  0.9 1.9 collective-permute-start
  2.8 13.9 %collective-permute-start.1 = (f32[5,2,2,128]{3,2,1,0:T(2,128)S(1)}, f32[5,2,2,128]{3,2,1,0:T(2,128)S(1)}, u32[]{:S(2)}, u32[]{:S(2)}) collective-permute-start(f32[5,2,2,128]{3,2,1,0:T(2,128)S(1)} %get-tuple-element.28), channel_id=1, source_target_pairs={{1,0},{2,1},{3,2},{4,3},{5,4},{6,5},{7,6},{8,7},{9,8},{10,9},{11,1... | collective-permute-start | bytes 30728 | tf_op jit(solution)/shard_map/ppermute | solution.py:22
  16.7 0.7 multiply_bitcast_fusion.1
  17.4 0.6 collective-permute-done.1
  18.2 3.4 %collective-permute-start.2 = (f32[5,2,12,2]{3,2,1,0:T(8,128)S(1)}, f32[5,2,12,2]{3,2,1,0:T(8,128)S(1)}, u32[]{:S(2)}, u32[]{:S(2)}) collective-permute-start(f32[5,2,12,2]{3,2,1,0:T(8,128)S(1)} %get-tuple-element.21), channel_id=1, source_target_pairs={{0,48},{48,96},{96,144},{144,192},{192,240},{240,288},{288,336},{3... | collective-permute-start | bytes 2888 | tf_op jit(solution)/shard_map/ppermute | solution.py:19
  21.6 6.4 %collective-permute-start.3 = (f32[5,2,12,2]{3,2,1,0:T(8,128)S(1)}, f32[5,2,12,2]{3,2,1,0:T(8,128)S(1)}, u32[]{:S(2)}, u32[]{:S(2)}) collective-permute-start(f32[5,2,12,2]{3,2,1,0:T(8,128)S(1)} %get-tuple-element.22), channel_id=1, source_target_pairs={{48,0},{96,48},{144,96},{192,144},{240,192},{288,240},{336,288},{3... | collective-permute-start | bytes 2888 | tf_op jit(solution)/shard_map/ppermute | solution.py:22
  28.4 1.6 collective-permute-done.3
  30.2 5.8 %collective-permute-start.4 = (f32[5,2,2,128]{3,2,1,0:T(2,128)S(1)}, f32[5,2,2,128]{3,2,1,0:T(2,128)S(1)}, u32[]{:S(2)}, u32[]{:S(2)}) collective-permute-start(f32[5,2,2,128]{3,2,1,0:T(2,128)S(1)} %get-tuple-element.25), channel_id=1, source_target_pairs={{0,1},{1,2},{2,3},{3,4},{4,5},{5,6},{6,7},{7,8},{8,9},{9,10},{10,1... | collective-permute-start | bytes 30728 | tf_op jit(solution)/shard_map/ppermute | solution.py:19
  36.0 5.8 %collective-permute-start.5 = (f32[5,2,2,128]{3,2,1,0:T(2,128)S(1)}, f32[5,2,2,128]{3,2,1,0:T(2,128)S(1)}, u32[]{:S(2)}, u32[]{:S(2)}) collective-permute-start(f32[5,2,2,128]{3,2,1,0:T(2,128)S(1)} %get-tuple-element.26), channel_id=1, source_target_pairs={{1,0},{2,1},{3,2},{4,3},{5,4},{6,5},{7,6},{8,7},{9,8},{10,9},{11,1... | collective-permute-start | bytes 30728 | tf_op jit(solution)/shard_map/ppermute | solution.py:22
  41.8 1.4 collective-permute-done.5
  43.3 1.9 collective-permute-start.6
  45.2 8.2 %collective-permute-start.7 = (f32[5,2,12,2]{3,2,1,0:T(8,128)S(1)}, f32[5,2,12,2]{3,2,1,0:T(8,128)S(1)}, u32[]{:S(2)}, u32[]{:S(2)}) collective-permute-start(f32[5,2,12,2]{3,2,1,0:T(8,128)S(1)} %get-tuple-element.20), channel_id=1, source_target_pairs={{48,0},{96,48},{144,96},{192,144},{240,192},{288,240},{336,288},{3... | collective-permute-start | bytes 2888 | tf_op jit(solution)/shard_map/ppermute | solution.py:22
  53.9 1.6 collective-permute-done.7
  55.7 1.9 collective-permute-start.8
  57.6 8.2 %collective-permute-done.8 = f32[5,2,8,128]{3,2,1,0:T(8,128)S(1)} collective-permute-done((f32[5,2,8,128]{3,2,1,0:T(8,128)S(1)}, f32[5,2,8,128]{3,2,1,0:T(8,128)S(1)}, u32[]{:S(2)}, u32[]{:S(2)}) %collective-permute-start.8) | collective-permute-done | bytes 40992 | tf_op jit(solution)/shard_map/ppermute | solution.py:30
  65.9 1.9 collective-permute-start.9
  67.8 8.2 %collective-permute-done.9 = f32[5,2,8,128]{3,2,1,0:T(8,128)S(1)} collective-permute-done((f32[5,2,8,128]{3,2,1,0:T(8,128)S(1)}, f32[5,2,8,128]{3,2,1,0:T(8,128)S(1)}, u32[]{:S(2)}, u32[]{:S(2)}) %collective-permute-start.9) | collective-permute-done | bytes 40992 | tf_op jit(solution)/shard_map/ppermute | solution.py:30
  76.1 1.9 collective-permute-start.10
  78.0 5.8 %collective-permute-done.10 = f32[5,2,8,128]{3,2,1,0:T(8,128)S(1)} collective-permute-done((f32[5,2,8,128]{3,2,1,0:T(8,128)S(1)}, f32[5,2,8,128]{3,2,1,0:T(8,128)S(1)}, u32[]{:S(2)}, u32[]{:S(2)}) %collective-permute-start.10) | collective-permute-done | bytes 40992 | tf_op jit(solution)/shard_map/ppermute | solution.py:30
  83.9 1.9 collective-permute-start.11
  85.8 4.9 %collective-permute-done.11 = f32[5,2,8,128]{3,2,1,0:T(8,128)S(1)} collective-permute-done((f32[5,2,8,128]{3,2,1,0:T(8,128)S(1)}, f32[5,2,8,128]{3,2,1,0:T(8,128)S(1)}, u32[]{:S(2)}, u32[]{:S(2)}) %collective-permute-start.11) | collective-permute-done | bytes 40992 | tf_op jit(solution)/shard_map/ppermute | solution.py:30
  90.7 1.9 collective-permute-start.12
  92.8 7.8 %collective-permute-done.12 = f32[5,2,8,128]{3,2,1,0:T(8,128)S(1)} collective-permute-done((f32[5,2,8,128]{3,2,1,0:T(8,128)S(1)}, f32[5,2,8,128]{3,2,1,0:T(8,128)S(1)}, u32[]{:S(2)}, u32[]{:S(2)}) %collective-permute-start.12) | collective-permute-done | bytes 40992 | tf_op jit(solution)/shard_map/ppermute | solution.py:30
  101.8 1.9 collective-permute-start.13
  103.7 9.7 %collective-permute-start.14 = (f32[5,2,2,128]{3,2,1,0:T(2,128)S(1)}, f32[5,2,2,128]{3,2,1,0:T(2,128)S(1)}, u32[]{:S(2)}, u32[]{:S(2)}) collective-permute-start(f32[5,2,2,128]{3,2,1,0:T(2,128)S(1)} %get-tuple-element.16), channel_id=1, source_target_pairs={{1,0},{2,1},{3,2},{4,3},{5,4},{6,5},{7,6},{8,7},{9,8},{10,9},{11,1... | collective-permute-start | bytes 30728 | tf_op jit(solution)/shard_map/ppermute | solution.py:22
  113.4 1.3 collective-permute-done.14
  114.9 1.9 collective-permute-start.15
  116.8 7.8 %collective-permute-start.16 = (f32[5,2,12,2]{3,2,1,0:T(8,128)S(1)}, f32[5,2,12,2]{3,2,1,0:T(8,128)S(1)}, u32[]{:S(2)}, u32[]{:S(2)}) collective-permute-start(f32[5,2,12,2]{3,2,1,0:T(8,128)S(1)} %get-tuple-element.14), channel_id=1, source_target_pairs={{48,0},{96,48},{144,96},{192,144},{240,192},{288,240},{336,288},{3... | collective-permute-start | bytes 2888 | tf_op jit(solution)/shard_map/ppermute | solution.py:22
  124.6 1.0 collective-permute-done.15
  125.7 1.4 collective-permute-done.16
  127.3 1.9 collective-permute-start.17
  129.3 9.7 %collective-permute-start.18 = (f32[5,2,2,128]{3,2,1,0:T(2,128)S(1)}, f32[5,2,2,128]{3,2,1,0:T(2,128)S(1)}, u32[]{:S(2)}, u32[]{:S(2)}) collective-permute-start(f32[5,2,2,128]{3,2,1,0:T(2,128)S(1)} %get-tuple-element.24), channel_id=1, source_target_pairs={{1,0},{2,1},{3,2},{4,3},{5,4},{6,5},{7,6},{8,7},{9,8},{10,9},{11,1... | collective-permute-start | bytes 30728 | tf_op jit(solution)/shard_map/ppermute | solution.py:22
  138.9 1.4 collective-permute-done.18
  140.4 1.9 collective-permute-start.19
  142.3 8.3 %collective-permute-start.20 = (f32[5,2,12,2]{3,2,1,0:T(8,128)S(1)}, f32[5,2,12,2]{3,2,1,0:T(8,128)S(1)}, u32[]{:S(2)}, u32[]{:S(2)}) collective-permute-start(f32[5,2,12,2]{3,2,1,0:T(8,128)S(1)} %get-tuple-element.12), channel_id=1, source_target_pairs={{48,0},{96,48},{144,96},{192,144},{240,192},{288,240},{336,288},{3... | collective-permute-start | bytes 2888 | tf_op jit(solution)/shard_map/ppermute | solution.py:22
  151.1 1.6 collective-permute-done.20
  152.8 1.9 collective-permute-start.21
  154.8 8.2 %collective-permute-done.21 = f32[5,2,8,128]{3,2,1,0:T(8,128)S(1)} collective-permute-done((f32[5,2,8,128]{3,2,1,0:T(8,128)S(1)}, f32[5,2,8,128]{3,2,1,0:T(8,128)S(1)}, u32[]{:S(2)}, u32[]{:S(2)}) %collective-permute-start.21) | collective-permute-done | bytes 40992 | tf_op jit(solution)/shard_map/ppermute | solution.py:30
  163.1 1.9 collective-permute-start.22
  165.0 8.2 %collective-permute-done.22 = f32[5,2,8,128]{3,2,1,0:T(8,128)S(1)} collective-permute-done((f32[5,2,8,128]{3,2,1,0:T(8,128)S(1)}, f32[5,2,8,128]{3,2,1,0:T(8,128)S(1)}, u32[]{:S(2)}, u32[]{:S(2)}) %collective-permute-start.22) | collective-permute-done | bytes 40992 | tf_op jit(solution)/shard_map/ppermute | solution.py:30
  173.2 1.9 collective-permute-start.23
  175.2 5.9 %collective-permute-done.23 = f32[5,2,8,128]{3,2,1,0:T(8,128)S(1)} collective-permute-done((f32[5,2,8,128]{3,2,1,0:T(8,128)S(1)}, f32[5,2,8,128]{3,2,1,0:T(8,128)S(1)}, u32[]{:S(2)}, u32[]{:S(2)}) %collective-permute-start.23) | collective-permute-done | bytes 40992 | tf_op jit(solution)/shard_map/ppermute | solution.py:30
  181.1 1.9 collective-permute-start.24
  183.0 4.9 %collective-permute-done.24 = f32[5,2,8,128]{3,2,1,0:T(8,128)S(1)} collective-permute-done((f32[5,2,8,128]{3,2,1,0:T(8,128)S(1)}, f32[5,2,8,128]{3,2,1,0:T(8,128)S(1)}, u32[]{:S(2)}, u32[]{:S(2)}) %collective-permute-start.24) | collective-permute-done | bytes 40992 | tf_op jit(solution)/shard_map/ppermute | solution.py:30
  188.0 1.9 collective-permute-start.25
  189.9 7.8 %collective-permute-done.25 = f32[5,2,8,128]{3,2,1,0:T(8,128)S(1)} collective-permute-done((f32[5,2,8,128]{3,2,1,0:T(8,128)S(1)}, f32[5,2,8,128]{3,2,1,0:T(8,128)S(1)}, u32[]{:S(2)}, u32[]{:S(2)}) %collective-permute-start.25) | collective-permute-done | bytes 40992 | tf_op jit(solution)/shard_map/ppermute | solution.py:30
  198.9 0.7 fusion.11
  (73 shorter events, 5.8 us)
Async XLA Ops:
  0.0 17.4 %copy-start = (f32[5,2,8,128]{3,2,1,0:T(8,128)S(1)}, f32[5,2,8,128]{3,2,1,0:T(8,128)}, u32[]{:S(2)}) copy-start(f32[5,2,8,128]{3,2,1,0:T(8,128)} %param.3) | copy-start | bytes 122884
  0.9 16.5 %collective-permute-start = (f32[5,2,2,128]{3,2,1,0:T(2,128)S(1)}, f32[5,2,2,128]{3,2,1,0:T(2,128)S(1)}, u32[]{:S(2)}, u32[]{:S(2)}) collective-permute-start(f32[5,2,2,128]{3,2,1,0:T(2,128)S(1)} %get-tuple-element.27), channel_id=1, source_target_pairs={{0,1},{1,2},{2,3},{3,4},{4,5},{5,6},{6,7},{7,8},{8,9},{9,10},{10,1... | collective-permute-start | bytes 30728 | tf_op jit(solution)/shard_map/ppermute | solution.py:19
  2.8 15.3 %collective-permute-start.1 = (f32[5,2,2,128]{3,2,1,0:T(2,128)S(1)}, f32[5,2,2,128]{3,2,1,0:T(2,128)S(1)}, u32[]{:S(2)}, u32[]{:S(2)}) collective-permute-start(f32[5,2,2,128]{3,2,1,0:T(2,128)S(1)} %get-tuple-element.28), channel_id=1, source_target_pairs={{1,0},{2,1},{3,2},{4,3},{5,4},{6,5},{7,6},{8,7},{9,8},{10,9},{11,1... | collective-permute-start | bytes 30728 | tf_op jit(solution)/shard_map/ppermute | solution.py:22
  18.2 10.2 %collective-permute-start.2 = (f32[5,2,12,2]{3,2,1,0:T(8,128)S(1)}, f32[5,2,12,2]{3,2,1,0:T(8,128)S(1)}, u32[]{:S(2)}, u32[]{:S(2)}) collective-permute-start(f32[5,2,12,2]{3,2,1,0:T(8,128)S(1)} %get-tuple-element.21), channel_id=1, source_target_pairs={{0,48},{48,96},{96,144},{144,192},{192,240},{240,288},{288,336},{3... | collective-permute-start | bytes 2888 | tf_op jit(solution)/shard_map/ppermute | solution.py:19
  21.6 8.4 %collective-permute-start.3 = (f32[5,2,12,2]{3,2,1,0:T(8,128)S(1)}, f32[5,2,12,2]{3,2,1,0:T(8,128)S(1)}, u32[]{:S(2)}, u32[]{:S(2)}) collective-permute-start(f32[5,2,12,2]{3,2,1,0:T(8,128)S(1)} %get-tuple-element.22), channel_id=1, source_target_pairs={{48,0},{96,48},{144,96},{192,144},{240,192},{288,240},{336,288},{3... | collective-permute-start | bytes 2888 | tf_op jit(solution)/shard_map/ppermute | solution.py:22
  30.2 11.6 %collective-permute-start.4 = (f32[5,2,2,128]{3,2,1,0:T(2,128)S(1)}, f32[5,2,2,128]{3,2,1,0:T(2,128)S(1)}, u32[]{:S(2)}, u32[]{:S(2)}) collective-permute-start(f32[5,2,2,128]{3,2,1,0:T(2,128)S(1)} %get-tuple-element.25), channel_id=1, source_target_pairs={{0,1},{1,2},{2,3},{3,4},{4,5},{5,6},{6,7},{7,8},{8,9},{9,10},{10,1... | collective-permute-start | bytes 30728 | tf_op jit(solution)/shard_map/ppermute | solution.py:19
  36.0 7.2 %collective-permute-start.5 = (f32[5,2,2,128]{3,2,1,0:T(2,128)S(1)}, f32[5,2,2,128]{3,2,1,0:T(2,128)S(1)}, u32[]{:S(2)}, u32[]{:S(2)}) collective-permute-start(f32[5,2,2,128]{3,2,1,0:T(2,128)S(1)} %get-tuple-element.26), channel_id=1, source_target_pairs={{1,0},{2,1},{3,2},{4,3},{5,4},{6,5},{7,6},{8,7},{9,8},{10,9},{11,1... | collective-permute-start | bytes 30728 | tf_op jit(solution)/shard_map/ppermute | solution.py:22
  43.3 10.1 %copy-start.1 = (s32[8]{0:T(128)S(1)}, s32[8]{0:T(128)}, u32[]{:S(2)}) copy-start(s32[8]{0:T(128)} %param.5) | copy-start | bytes 100
  43.3 10.6 %collective-permute-start.6 = (f32[5,2,12,2]{3,2,1,0:T(8,128)S(1)}, f32[5,2,12,2]{3,2,1,0:T(8,128)S(1)}, u32[]{:S(2)}, u32[]{:S(2)}) collective-permute-start(f32[5,2,12,2]{3,2,1,0:T(8,128)S(1)} %get-tuple-element.19), channel_id=1, source_target_pairs={{0,48},{48,96},{96,144},{144,192},{192,240},{240,288},{288,336},{3... | collective-permute-start | bytes 2888 | tf_op jit(solution)/shard_map/ppermute | solution.py:19
  45.2 10.2 %collective-permute-start.7 = (f32[5,2,12,2]{3,2,1,0:T(8,128)S(1)}, f32[5,2,12,2]{3,2,1,0:T(8,128)S(1)}, u32[]{:S(2)}, u32[]{:S(2)}) collective-permute-start(f32[5,2,12,2]{3,2,1,0:T(8,128)S(1)} %get-tuple-element.20), channel_id=1, source_target_pairs={{48,0},{96,48},{144,96},{192,144},{240,192},{288,240},{336,288},{3... | collective-permute-start | bytes 2888 | tf_op jit(solution)/shard_map/ppermute | solution.py:22
  55.7 10.2 %collective-permute-start.8 = (f32[5,2,8,128]{3,2,1,0:T(8,128)S(1)}, f32[5,2,8,128]{3,2,1,0:T(8,128)S(1)}, u32[]{:S(2)}, u32[]{:S(2)}) collective-permute-start(f32[5,2,8,128]{3,2,1,0:T(8,128)S(1)} %fusion.16), channel_id=1, source_target_pairs={{720,0},{0,48},{48,96},{96,144},{144,192},{192,240},{240,288},{288... | collective-permute-start | bytes 122888 | tf_op jit(solution)/shard_map/ppermute | solution.py:30
  65.9 10.2 %collective-permute-start.9 = (f32[5,2,8,128]{3,2,1,0:T(8,128)S(1)}, f32[5,2,8,128]{3,2,1,0:T(8,128)S(1)}, u32[]{:S(2)}, u32[]{:S(2)}) collective-permute-start(f32[5,2,8,128]{3,2,1,0:T(8,128)S(1)} %broadcast_select_fusion.1), channel_id=1, source_target_pairs={{672,0},{720,48},{0,96},{48,144},{96,192},{144,240},{192,288},{240... | collective-permute-start | bytes 122888 | tf_op jit(solution)/shard_map/ppermute | solution.py:30
  76.1 7.7 %collective-permute-start.10 = (f32[5,2,8,128]{3,2,1,0:T(8,128)S(1)}, f32[5,2,8,128]{3,2,1,0:T(8,128)S(1)}, u32[]{:S(2)}, u32[]{:S(2)}) collective-permute-start(f32[5,2,8,128]{3,2,1,0:T(8,128)S(1)} %broadcast_select_fusion.3), channel_id=1, source_target_pairs={{576,0},{624,48},{672,96},{720,144},{0,192},{48,240},{96,288},{144... | collective-permute-start | bytes 122888 | tf_op jit(solution)/shard_map/ppermute | solution.py:30
  83.9 6.8 %collective-permute-start.11 = (f32[5,2,8,128]{3,2,1,0:T(8,128)S(1)}, f32[5,2,8,128]{3,2,1,0:T(8,128)S(1)}, u32[]{:S(2)}, u32[]{:S(2)}) collective-permute-start(f32[5,2,8,128]{3,2,1,0:T(8,128)S(1)} %broadcast_select_fusion.5), channel_id=1, source_target_pairs={{384,0},{432,48},{480,96},{528,144},{576,192},{624,240},{672,288},... | collective-permute-start | bytes 122888 | tf_op jit(solution)/shard_map/ppermute | solution.py:30
  90.7 9.8 %collective-permute-start.12 = (f32[5,2,8,128]{3,2,1,0:T(8,128)S(1)}, f32[5,2,8,128]{3,2,1,0:T(8,128)S(1)}, u32[]{:S(2)}, u32[]{:S(2)}) collective-permute-start(f32[5,2,8,128]{3,2,1,0:T(8,128)S(1)} %broadcast_select_fusion.7), channel_id=1, source_target_pairs={{720,0},{0,48},{48,96},{96,144},{144,192},{192,240},{240,288},{288... | collective-permute-start | bytes 122888 | tf_op jit(solution)/shard_map/ppermute | solution.py:30
  101.8 11.6 %collective-permute-start.13 = (f32[5,2,2,128]{3,2,1,0:T(2,128)S(1)}, f32[5,2,2,128]{3,2,1,0:T(2,128)S(1)}, u32[]{:S(2)}, u32[]{:S(2)}) collective-permute-start(f32[5,2,2,128]{3,2,1,0:T(2,128)S(1)} %get-tuple-element.15), channel_id=1, source_target_pairs={{0,1},{1,2},{2,3},{3,4},{4,5},{5,6},{6,7},{7,8},{8,9},{9,10},{10,1... | collective-permute-start | bytes 30728 | tf_op jit(solution)/shard_map/ppermute | solution.py:19
  103.7 11.0 %collective-permute-start.14 = (f32[5,2,2,128]{3,2,1,0:T(2,128)S(1)}, f32[5,2,2,128]{3,2,1,0:T(2,128)S(1)}, u32[]{:S(2)}, u32[]{:S(2)}) collective-permute-start(f32[5,2,2,128]{3,2,1,0:T(2,128)S(1)} %get-tuple-element.16), channel_id=1, source_target_pairs={{1,0},{2,1},{3,2},{4,3},{5,4},{6,5},{7,6},{8,7},{9,8},{10,9},{11,1... | collective-permute-start | bytes 30728 | tf_op jit(solution)/shard_map/ppermute | solution.py:22
  114.9 10.8 %collective-permute-start.15 = (f32[5,2,12,2]{3,2,1,0:T(8,128)S(1)}, f32[5,2,12,2]{3,2,1,0:T(8,128)S(1)}, u32[]{:S(2)}, u32[]{:S(2)}) collective-permute-start(f32[5,2,12,2]{3,2,1,0:T(8,128)S(1)} %get-tuple-element.13), channel_id=1, source_target_pairs={{0,48},{48,96},{96,144},{144,192},{192,240},{240,288},{288,336},{3... | collective-permute-start | bytes 2888 | tf_op jit(solution)/shard_map/ppermute | solution.py:19
  116.8 10.3 %collective-permute-start.16 = (f32[5,2,12,2]{3,2,1,0:T(8,128)S(1)}, f32[5,2,12,2]{3,2,1,0:T(8,128)S(1)}, u32[]{:S(2)}, u32[]{:S(2)}) collective-permute-start(f32[5,2,12,2]{3,2,1,0:T(8,128)S(1)} %get-tuple-element.14), channel_id=1, source_target_pairs={{48,0},{96,48},{144,96},{192,144},{240,192},{288,240},{336,288},{3... | collective-permute-start | bytes 2888 | tf_op jit(solution)/shard_map/ppermute | solution.py:22
  127.3 11.6 %collective-permute-start.17 = (f32[5,2,2,128]{3,2,1,0:T(2,128)S(1)}, f32[5,2,2,128]{3,2,1,0:T(2,128)S(1)}, u32[]{:S(2)}, u32[]{:S(2)}) collective-permute-start(f32[5,2,2,128]{3,2,1,0:T(2,128)S(1)} %get-tuple-element.23), channel_id=1, source_target_pairs={{0,1},{1,2},{2,3},{3,4},{4,5},{5,6},{6,7},{7,8},{8,9},{9,10},{10,1... | collective-permute-start | bytes 30728 | tf_op jit(solution)/shard_map/ppermute | solution.py:19
  129.3 11.0 %collective-permute-start.18 = (f32[5,2,2,128]{3,2,1,0:T(2,128)S(1)}, f32[5,2,2,128]{3,2,1,0:T(2,128)S(1)}, u32[]{:S(2)}, u32[]{:S(2)}) collective-permute-start(f32[5,2,2,128]{3,2,1,0:T(2,128)S(1)} %get-tuple-element.24), channel_id=1, source_target_pairs={{1,0},{2,1},{3,2},{4,3},{5,4},{6,5},{7,6},{8,7},{9,8},{10,9},{11,1... | collective-permute-start | bytes 30728 | tf_op jit(solution)/shard_map/ppermute | solution.py:22
  140.4 10.7 %collective-permute-start.19 = (f32[5,2,12,2]{3,2,1,0:T(8,128)S(1)}, f32[5,2,12,2]{3,2,1,0:T(8,128)S(1)}, u32[]{:S(2)}, u32[]{:S(2)}) collective-permute-start(f32[5,2,12,2]{3,2,1,0:T(8,128)S(1)} %get-tuple-element.11), channel_id=1, source_target_pairs={{0,48},{48,96},{96,144},{144,192},{192,240},{240,288},{288,336},{3... | collective-permute-start | bytes 2888 | tf_op jit(solution)/shard_map/ppermute | solution.py:19
  142.3 10.3 %collective-permute-start.20 = (f32[5,2,12,2]{3,2,1,0:T(8,128)S(1)}, f32[5,2,12,2]{3,2,1,0:T(8,128)S(1)}, u32[]{:S(2)}, u32[]{:S(2)}) collective-permute-start(f32[5,2,12,2]{3,2,1,0:T(8,128)S(1)} %get-tuple-element.12), channel_id=1, source_target_pairs={{48,0},{96,48},{144,96},{192,144},{240,192},{288,240},{336,288},{3... | collective-permute-start | bytes 2888 | tf_op jit(solution)/shard_map/ppermute | solution.py:22
  152.8 10.2 %collective-permute-start.21 = (f32[5,2,8,128]{3,2,1,0:T(8,128)S(1)}, f32[5,2,8,128]{3,2,1,0:T(8,128)S(1)}, u32[]{:S(2)}, u32[]{:S(2)}) collective-permute-start(f32[5,2,8,128]{3,2,1,0:T(8,128)S(1)} %fusion.13), channel_id=1, source_target_pairs={{720,0},{0,48},{48,96},{96,144},{144,192},{192,240},{240,288},{288... | collective-permute-start | bytes 122888 | tf_op jit(solution)/shard_map/ppermute | solution.py:30
  163.1 10.1 %collective-permute-start.22 = (f32[5,2,8,128]{3,2,1,0:T(8,128)S(1)}, f32[5,2,8,128]{3,2,1,0:T(8,128)S(1)}, u32[]{:S(2)}, u32[]{:S(2)}) collective-permute-start(f32[5,2,8,128]{3,2,1,0:T(8,128)S(1)} %broadcast_select_fusion), channel_id=1, source_target_pairs={{672,0},{720,48},{0,96},{48,144},{96,192},{144,240},{192,288},{240... | collective-permute-start | bytes 122888 | tf_op jit(solution)/shard_map/ppermute | solution.py:30
  173.2 7.8 %collective-permute-start.23 = (f32[5,2,8,128]{3,2,1,0:T(8,128)S(1)}, f32[5,2,8,128]{3,2,1,0:T(8,128)S(1)}, u32[]{:S(2)}, u32[]{:S(2)}) collective-permute-start(f32[5,2,8,128]{3,2,1,0:T(8,128)S(1)} %broadcast_select_fusion.2), channel_id=1, source_target_pairs={{576,0},{624,48},{672,96},{720,144},{0,192},{48,240},{96,288},{144... | collective-permute-start | bytes 122888 | tf_op jit(solution)/shard_map/ppermute | solution.py:30
  181.1 6.8 %collective-permute-start.24 = (f32[5,2,8,128]{3,2,1,0:T(8,128)S(1)}, f32[5,2,8,128]{3,2,1,0:T(8,128)S(1)}, u32[]{:S(2)}, u32[]{:S(2)}) collective-permute-start(f32[5,2,8,128]{3,2,1,0:T(8,128)S(1)} %broadcast_select_fusion.4), channel_id=1, source_target_pairs={{384,0},{432,48},{480,96},{528,144},{576,192},{624,240},{672,288},... | collective-permute-start | bytes 122888 | tf_op jit(solution)/shard_map/ppermute | solution.py:30
  188.0 9.8 %collective-permute-start.25 = (f32[5,2,8,128]{3,2,1,0:T(8,128)S(1)}, f32[5,2,8,128]{3,2,1,0:T(8,128)S(1)}, u32[]{:S(2)}, u32[]{:S(2)}) collective-permute-start(f32[5,2,8,128]{3,2,1,0:T(8,128)S(1)} %broadcast_select_fusion.6), channel_id=1, source_target_pairs={{720,0},{0,48},{48,96},{96,144},{144,192},{192,240},{240,288},{288... | collective-permute-start | bytes 122888 | tf_op jit(solution)/shard_map/ppermute | solution.py:30
where the time goes:
time: 201 us; the launch traced here: 200 us
  starting transfers between devices  109 us (54%)
  waiting for transfers between devices  83 us (41%)
  other arithmetic  4.33 us (2%)
  local copies, waits for them, and re-layouts  2.34 us (1%)
    ppermute x10, waiting for transfers between devices, from_behind(): return lax.ppermute(block, axis, route)  69.8 us
    ppermute x8, starting transfers between devices, with_halo(): lax.ppermute(lax.slice_in_dim(block, 0, width, axis=dim), axis, backward)  69.6 us
    ppermute x8, starting transfers between devices, with_halo(): lax.ppermute(lax.slice_in_dim(block, block.shape[dim] - width, None, axis...  20.7 us
    ppermute x10, starting transfers between devices, from_behind(): return lax.ppermute(block, axis, route)  19.1 us
    ppermute x8, waiting for transfers between devices, with_halo(): lax.ppermute(lax.slice_in_dim(block, 0, width, axis=dim), axis, backward)  10.8 us
  transfers between devices with their start and end apart: 26, of which 22 were waited for; matrix products, arithmetic and copies ran while one was open for 0% of the time, Pallas kernels for 0%

commit v1 on v0

v1 whole, which is shorter than its diff:
```python
import jax
import jax.numpy as jnp
from jax import lax
from jax.experimental import pallas as pl
from jax.experimental.pallas import tpu as pltpu
from jax.sharding import PartitionSpec as P

STEPS = 2
VISCOSITY = 0.05
LANES = 128
ROWS = 8


def around(row, lane):
    blocks = row.shape[0]
    behind = pltpu.roll(row, 1, axis=0)
    ahead = pltpu.roll(row, blocks - 1, axis=0)
    m2 = pltpu.roll(jnp.where(lane >= LANES - 2, behind, row), 2, axis=1)
    m1 = pltpu.roll(jnp.where(lane >= LANES - 1, behind, row), 1, axis=1)
    p1 = pltpu.roll(jnp.where(lane < 1, ahead, row), LANES - 1, axis=1)
    p2 = pltpu.roll(jnp.where(lane < 2, ahead, row), LANES - 2, axis=1)
    return m2, m1, p1, p2


def tendency(load, r, v_r, v_p, lane):
    centre = load(r)
    m2, m1, p1, p2 = around(centre, lane)
    r_m2, r_m1, r_p1, r_p2 = load(r - 2), load(r - 1), load(r + 1), load(r + 2)
    near = (m1 + p1) + (r_m1 + r_p1)
    far = (m2 + p2) + (r_m2 + r_p2)
    slope_p = (p1 - m1) * (8.0 / 12.0) - (p2 - m2) * (1.0 / 12.0)
    slope_r = (r_p1 - r_m1) * (8.0 / 12.0) - (r_p2 - r_m2) * (1.0 / 12.0)
    scale = VISCOSITY / 12.0
    curve = near * (16.0 * scale) - far * scale - centre * (60.0 * scale)
    return centre, curve - v_p * slope_p - v_r * slope_r


def steps_kernel(meta, low, own, high, out, state, section, ring):
    blocks = own.shape[0] // (3 * ROWS)
    lane = lax.broadcasted_iota(jnp.int32, (blocks, LANES), 1)
    has_low = meta[2 * ROWS] > 0
    has_high = meta[2 * ROWS + 1] > 0

    def source(r):
        return (low, own, high)[r // ROWS], r % ROWS

    def arrived(r, part):
        ref, local = source(r)
        return ref[pl.ds(part * ROWS + local, blocks, stride=3 * ROWS), :]

    def inside(r, value):
        if r < ROWS:
            return jnp.where(has_low, value, 0.0)
        if r >= 2 * ROWS:
            return jnp.where(has_high, value, 0.0)
        return value

    def shifted(r, value):
        ring[r, :blocks, :] = value
        ring[r, blocks:, :] = value
        offset = meta[r - ROWS // 2]
        hops = offset // LANES
        rest = offset % LANES
        near = ring[r, pl.ds(blocks - hops, blocks), :]
        far = ring[r, pl.ds(blocks - 1 - hops, blocks), :]
        return pltpu.roll(jnp.where(lane < LANES - rest, near, far), rest, axis=1)

    for r in range(3 * ROWS):
        state[r] = arrived(r, 0)
    margin = 0
    for step in range(STEPS):
        for r in range(margin + 2, 3 * ROWS - margin - 2):
            centre, change = tendency(lambda k: state[k], r, arrived(r, 1), arrived(r, 2), lane)
            section[r] = inside(r, centre + change)
        for r in range(margin + 4, 3 * ROWS - margin - 4):
            centre, change = tendency(lambda k: section[k], r, arrived(r, 1), arrived(r, 2), lane)
            value = shifted(r, inside(r, 0.5 * (state[r] + centre + change)))
            if step + 1 < STEPS:
                state[r] = value
            else:
                out[pl.ds(r - ROWS, blocks, stride=ROWS), :] = value
        margin += 4


def shards(fields, velocity, offsets):
    slabs = fields.shape[0] * fields.shape[1]
    blocks = lax.axis_size("az")
    count = lax.axis_size("rad")
    forward = [(i, i + 1) for i in range(count - 1)]
    backward = [(j, i) for i, j in forward]
    offs_low = lax.ppermute(offsets, "rad", forward)
    offs_high = lax.ppermute(offsets, "rad", backward)
    place = lax.axis_index("rad")
    flags = jnp.stack([(place > 0).astype(jnp.int32), (place < count - 1).astype(jnp.int32)])
    meta = jnp.concatenate([offs_low[ROWS // 2 :], offsets, offs_high[: ROWS // 2], flags])

    sent = jnp.pad(fields.reshape(slabs, ROWS, LANES), ((0, blocks - slabs), (0, 0), (0, 0)))
    speeds = jnp.broadcast_to(velocity.reshape(1, 2 * ROWS, LANES), (blocks, 2 * ROWS, LANES))
    sent = jnp.concatenate([sent, speeds], axis=1)
    own = lax.all_to_all(sent, "az", 0, 0, tiled=True)
    low = lax.ppermute(own, "rad", forward)
    high = lax.ppermute(own, "rad", backward)
    flat = (blocks * 3 * ROWS, LANES)
    vmem = pl.BlockSpec(memory_space=pltpu.VMEM)
    done = pl.pallas_call(
        steps_kernel,
        out_shape=jax.ShapeDtypeStruct((blocks * ROWS, LANES), jnp.float32),
        in_specs=[pl.BlockSpec(memory_space=pltpu.SMEM), vmem, vmem, vmem],
        out_specs=vmem,
        scratch_shapes=[
            pltpu.VMEM((3 * ROWS, blocks, LANES), jnp.float32),
            pltpu.VMEM((3 * ROWS, blocks, LANES), jnp.float32),
            pltpu.VMEM((3 * ROWS, 2 * blocks, LANES), jnp.float32),
        ],
        name="disc_steps",
    )(meta, low.reshape(flat), own.reshape(flat), high.reshape(flat))
    back = lax.all_to_all(done.reshape(blocks, ROWS, LANES), "az", 0, 0, tiled=True)
    return back[:slabs].reshape(fields.shape)


def solution(mesh):
    placed = (P(None, None, "rad", "az"), P(None, "rad", "az"), P("rad"))
    return jax.shard_map(
        shards, mesh=mesh, in_specs=placed, out_specs=P(None, None, "rad", "az"), check_vma=False
    )
```

time: 201 us -> 67.1 us (0.33)
  the two profiles are of different devices: /device:TPU:32 before, /device:TPU:40 now
where the time goes in v1:
time: 67.1 us; the launch traced here: 66.8 us
  blocking collectives  35.5 us (53%)
  starting transfers between devices  22.9 us (34%)
  Pallas kernels  3.79 us (6%)
  local copies, waits for them, and re-layouts  2.78 us (4%)
  waiting for transfers between devices  1.67 us (2%)
    all_to_all x1, blocking collectives, shards(): own = lax.all_to_all(sent, 'az', 0, 0, tiled=True)  19.3 us
    all_to_all x1, blocking collectives, shards(): lax.all_to_all(done.reshape(blocks, ROWS, LANES), 'az', 0, 0, tiled=True)  16.2 us
    ppermute x1, starting transfers between devices, shards(): high = lax.ppermute(own, 'rad', backward)  10.6 us
    ppermute x1, starting transfers between devices, shards(): offs_high = lax.ppermute(offsets, 'rad', backward)  8.38 us
    pallas_call x1, Pallas kernels, shards(): pl.pallas_call(steps_kernel, out_shape=jax.ShapeDtypeStruct((blocks * ROW...  3.79 us
    ppermute x1, starting transfers between devices, shards(): offs_low = lax.ppermute(offsets, 'rad', forward)  1.99 us
    ppermute x1, starting transfers between devices, shards(): low = lax.ppermute(own, 'rad', forward)  1.92 us
    ppermute x1, waiting for transfers between devices, shards(): offs_low = lax.ppermute(offsets, 'rad', forward)  1.67 us
  transfers between devices with their start and end apart: 4, of which 1 were waited for; matrix products, arithmetic and copies ran while one was open for 1% of the time, Pallas kernels for 0%

profile of v1, /device:TPU:40, one launch (start us, length us, event | category | flops | bytes accessed | tf_op | source)
XLA Modules:
  0.0 66.8 jit_solution(16132086328767614388)
XLA Ops:
  0.0 0.0 copy-start.3
  0.0 0.7 %broadcast_in_dim.8 = f32[16,16,128]{2,1,0:T(8,128)S(1)} broadcast(f32[16,128]{1,0:T(8,128)} %bitcast.15), dimensions={1,2} | broadcast | bytes 139264 | tf_op jit(solution)/shard_map/broadcast_in_dim | solution.py:98
  0.7 0.1 copy-done.3
  0.8 0.0 copy-start.4
  0.8 19.3 %all_to_all.10 = f32[16,24,128]{2,1,0:T(8,128)S(1)} all-to-all(f32[16,24,128]{2,1,0:T(8,128)S(1)} %select_maximum_fusion), channel_id=1, replica_groups=mesh['az'=16,'rad'=48] {'az'}, dimensions={0} | all-to-all | bytes 393216 | tf_op jit(solution)/shard_map/all_to_all | solution.py:100
  20.1 0.0 copy-start
  20.1 10.6 %collective-permute-start.3 = (f32[16,24,128]{2,1,0:T(8,128)S(1)}, f32[16,24,128]{2,1,0:T(8,128)S(1)}, u32[]{:S(2)}, u32[]{:S(2)}) collective-permute-start(f32[16,24,128]{2,1,0:T(8,128)S(1)} %all_to_all.10), channel_id=1, source_target_pairs={{1,0},{2,1},{3,2},{4,3},{5,4},{6,5},{7,6},{8,7},{9,8},{10,9},{11,1... | collective-permute-start | bytes 589832 | tf_op jit(solution)/shard_map/ppermute | solution.py:102
  30.7 1.9 %collective-permute-start.2 = (f32[16,24,128]{2,1,0:T(8,128)S(1)}, f32[16,24,128]{2,1,0:T(8,128)S(1)}, u32[]{:S(2)}, u32[]{:S(2)}) collective-permute-start(f32[16,24,128]{2,1,0:T(8,128)S(1)} %all_to_all.10), channel_id=1, source_target_pairs={{0,1},{1,2},{2,3},{3,4},{4,5},{5,6},{6,7},{7,8},{8,9},{9,10},{10,1... | collective-permute-start | bytes 589832 | tf_op jit(solution)/shard_map/ppermute | solution.py:101
  32.7 0.0 copy-done.4
  32.7 2.0 %collective-permute-start = (s32[8]{0:T(128)S(1)}, s32[8]{0:T(128)S(1)}, u32[]{:S(2)}, u32[]{:S(2)}) collective-permute-start(s32[8]{0:T(128)S(1)} %copy-done.4), channel_id=1, source_target_pairs={{0,1},{1,2},{2,3},{3,4},{4,5},{5,6},{6,7},{7,8},{8,9},{9,10},{10,1... | collective-permute-start | bytes 104 | tf_op jit(solution)/shard_map/ppermute | solution.py:91
  34.7 8.4 %collective-permute-start.1 = (s32[8]{0:T(128)S(1)}, s32[8]{0:T(128)S(1)}, u32[]{:S(2)}, u32[]{:S(2)}) collective-permute-start(s32[8]{0:T(128)S(1)} %copy-done.4), channel_id=1, source_target_pairs={{1,0},{2,1},{3,2},{4,3},{5,4},{6,5},{7,6},{8,7},{9,8},{10,9},{11,1... | collective-permute-start | bytes 104 | tf_op jit(solution)/shard_map/ppermute | solution.py:92
  43.1 1.7 %collective-permute-done = s32[8]{0:T(128)S(1)} collective-permute-done((s32[8]{0:T(128)S(1)}, s32[8]{0:T(128)S(1)}, u32[]{:S(2)}, u32[]{:S(2)}) %collective-permute-start) | collective-permute-done | bytes 64 | tf_op jit(solution)/shard_map/ppermute | solution.py:91
  44.7 0.1 slice.9
  44.8 0.0 collective-permute-done.1
  44.8 0.6 concatenate.6.meta
  45.4 0.0 collective-permute-done.3
  45.4 0.0 copy-start.1
  45.4 0.0 collective-permute-done.2
  45.4 0.0 copy-start.2
  45.4 0.0 copy-done
  45.4 0.6 copy-done.1
  46.1 0.1 copy-done.2
  46.1 3.8 %disc_steps.1 = f32[128,128]{1,0:T(8,128)} custom-call(s32[18]{0:T(128)} %concatenate.6.meta, f32[384,128]{1,0:T(8,128)} %bitcast.13, f32[384,128]{1,0:T(8,128)} %bitcast.10, f32[384,128]{1,0:T(8,128)} %bitcast.12), custom_call_target="tpu_custom_call" | custom-call | tf_op jit(solution)/shard_map/disc_steps/pallas_call | solution.py:105
  49.9 16.2 %all_to_all.11 = f32[16,8,128]{2,1,0:T(8,128)S(1)} all-to-all(f32[16,8,128]{2,1,0:T(8,128)} %bitcast.11), channel_id=1, replica_groups=mesh['az'=16,'rad'=48] {'az'}, dimensions={0} | all-to-all | bytes 131072 | tf_op jit(solution)/shard_map/all_to_all | solution.py:117
  66.1 0.6 slice.12
  (1 shorter events, 0.0 us)
Async XLA Ops:
  0.0 0.8 %copy-start.3 = (f32[5,2,8,128]{3,2,1,0:T(8,128)S(1)}, f32[5,2,8,128]{3,2,1,0:T(8,128)}, u32[]{:S(2)}) copy-start(f32[5,2,8,128]{3,2,1,0:T(8,128)} %param.3) | copy-start | bytes 122884
  0.8 31.8 %copy-start.4 = (s32[8]{0:T(128)S(1)}, s32[8]{0:T(128)}, u32[]{:S(2)}) copy-start(s32[8]{0:T(128)} %param.5) | copy-start | bytes 100
  20.1 25.3 %copy-start = (f32[16,24,128]{2,1,0:T(8,128)}, f32[16,24,128]{2,1,0:T(8,128)S(1)}, u32[]{:S(2)}) copy-start(f32[16,24,128]{2,1,0:T(8,128)S(1)} %all_to_all.10) | copy-start | bytes 589828
  20.1 25.3 %collective-permute-start.3 = (f32[16,24,128]{2,1,0:T(8,128)S(1)}, f32[16,24,128]{2,1,0:T(8,128)S(1)}, u32[]{:S(2)}, u32[]{:S(2)}) collective-permute-start(f32[16,24,128]{2,1,0:T(8,128)S(1)} %all_to_all.10), channel_id=1, source_target_pairs={{1,0},{2,1},{3,2},{4,3},{5,4},{6,5},{7,6},{8,7},{9,8},{10,9},{11,1... | collective-permute-start | bytes 589832 | tf_op jit(solution)/shard_map/ppermute | solution.py:102
  30.7 14.7 %collective-permute-start.2 = (f32[16,24,128]{2,1,0:T(8,128)S(1)}, f32[16,24,128]{2,1,0:T(8,128)S(1)}, u32[]{:S(2)}, u32[]{:S(2)}) collective-permute-start(f32[16,24,128]{2,1,0:T(8,128)S(1)} %all_to_all.10), channel_id=1, source_target_pairs={{0,1},{1,2},{2,3},{3,4},{4,5},{5,6},{6,7},{7,8},{8,9},{9,10},{10,1... | collective-permute-start | bytes 589832 | tf_op jit(solution)/shard_map/ppermute | solution.py:101
  32.7 12.1 %collective-permute-start = (s32[8]{0:T(128)S(1)}, s32[8]{0:T(128)S(1)}, u32[]{:S(2)}, u32[]{:S(2)}) collective-permute-start(s32[8]{0:T(128)S(1)} %copy-done.4), channel_id=1, source_target_pairs={{0,1},{1,2},{2,3},{3,4},{4,5},{5,6},{6,7},{7,8},{8,9},{9,10},{10,1... | collective-permute-start | bytes 104 | tf_op jit(solution)/shard_map/ppermute | solution.py:91
  34.7 10.1 %collective-permute-start.1 = (s32[8]{0:T(128)S(1)}, s32[8]{0:T(128)S(1)}, u32[]{:S(2)}, u32[]{:S(2)}) collective-permute-start(s32[8]{0:T(128)S(1)} %copy-done.4), channel_id=1, source_target_pairs={{1,0},{2,1},{3,2},{4,3},{5,4},{6,5},{7,6},{8,7},{9,8},{10,9},{11,1... | collective-permute-start | bytes 104 | tf_op jit(solution)/shard_map/ppermute | solution.py:92
  45.4 0.7 %copy-start.1 = (f32[16,24,128]{2,1,0:T(8,128)}, f32[16,24,128]{2,1,0:T(8,128)S(1)}, u32[]{:S(2)}) copy-start(f32[16,24,128]{2,1,0:T(8,128)S(1)} %collective-permute-done.3) | copy-start | bytes 589828
  45.4 0.7 %copy-start.2 = (f32[16,24,128]{2,1,0:T(8,128)}, f32[16,24,128]{2,1,0:T(8,128)S(1)}, u32[]{:S(2)}) copy-start(f32[16,24,128]{2,1,0:T(8,128)S(1)} %collective-permute-done.2) | copy-start | bytes 589828

commit v2 on v1

v2 whole, which is shorter than its diff:
```python
import jax
import jax.numpy as jnp
from jax import lax
from jax.experimental import pallas as pl
from jax.experimental.pallas import tpu as pltpu
from jax.sharding import PartitionSpec as P

STEPS = 2
VISCOSITY = 0.05
LANES = 128
ROWS = 8
MARGIN = 4 * STEPS


def around(row, lane):
    blocks = row.shape[0]
    behind = pltpu.roll(row, 1, axis=0)
    ahead = pltpu.roll(row, blocks - 1, axis=0)
    m2 = pltpu.roll(jnp.where(lane >= LANES - 2, behind, row), 2, axis=1)
    m1 = pltpu.roll(jnp.where(lane >= LANES - 1, behind, row), 1, axis=1)
    p1 = pltpu.roll(jnp.where(lane < 1, ahead, row), LANES - 1, axis=1)
    p2 = pltpu.roll(jnp.where(lane < 2, ahead, row), LANES - 2, axis=1)
    return m2, m1, p1, p2


def tendency(field, r, v_r, v_p, lane):
    centre = field[r]
    m2, m1, p1, p2 = around(centre, lane)
    r_m2, r_m1, r_p1, r_p2 = field[r - 2], field[r - 1], field[r + 1], field[r + 2]
    near = (m1 + p1) + (r_m1 + r_p1)
    far = (m2 + p2) + (r_m2 + r_p2)
    slope_p = (p1 - m1) * (8.0 / 12.0) - (p2 - m2) * (1.0 / 12.0)
    slope_r = (r_p1 - r_m1) * (8.0 / 12.0) - (r_p2 - r_m2) * (1.0 / 12.0)
    scale = VISCOSITY / 12.0
    curve = near * (16.0 * scale) - far * scale - centre * (60.0 * scale)
    return centre, curve - v_p * slope_p - v_r * slope_r


def gather_kernel(offsets, arrived, block):
    blocks = arrived.shape[0] // (3 * ROWS)
    for k in range(3 * ROWS):
        block[pl.ds(k * blocks, blocks), :] = arrived[pl.ds(k, blocks, stride=3 * ROWS), :]
    line = lax.broadcasted_iota(jnp.int32, (ROWS, LANES), 0)
    shifts = jnp.zeros((ROWS, LANES), jnp.int32)
    for k in range(ROWS):
        shifts = jnp.where(line == k, offsets[k], shifts)
    block[pl.ds(3 * ROWS * blocks, ROWS), :] = shifts.astype(jnp.float32)


def steps_kernel(offsets, own, chip, cross, out, state, section, ring, speed, shifts, sem):
    size = own.shape[0]
    blocks = (size - ROWS) // (3 * ROWS)
    lane = lax.broadcasted_iota(jnp.int32, (blocks, LANES), 1)
    place = lax.axis_index("rad")
    upper = place % 2
    theirs = upper * size
    tails = [
        pltpu.make_async_copy(chip.at[pl.ds(size - ROWS, ROWS)], shifts.at[0], sem.at[0]),
        pltpu.make_async_copy(cross.at[pl.ds(theirs + size - ROWS, ROWS)], shifts.at[1], sem.at[1]),
    ]
    for tail in tails:
        tail.start()
    has_low = place > 0
    has_high = place < lax.axis_size("rad") - 1

    def tidy(part, k, value):
        if part == 0:
            return jnp.where(has_low, value, 0.0)
        return jnp.where(has_high, value, 0.0)

    for k in range(3 * ROWS):
        row = pl.ds(k * blocks, blocks)
        from_chip = chip[row, :]
        from_cross = cross[pl.ds(theirs + k * blocks, blocks), :]
        low = jnp.where(upper == 0, from_cross, from_chip)
        high = jnp.where(upper == 0, from_chip, from_cross)
        kind, local = k // ROWS, k % ROWS
        if kind == 0:
            state[local] = tidy(0, k, low)
            state[ROWS + local] = own[row, :]
            state[2 * ROWS + local] = tidy(1, k, high)
        else:
            speed[kind - 1, local] = low
            speed[kind - 1, ROWS + local] = own[row, :]
            speed[kind - 1, 2 * ROWS + local] = high

    def inside(r, value):
        if r < ROWS:
            return tidy(0, r, value)
        if r >= 2 * ROWS:
            return tidy(1, r, value)
        return value

    def shift_of(r):
        local = r % ROWS
        if r // ROWS == 1:
            return offsets[local]
        from_chip = shifts[0, local, 0]
        from_cross = shifts[1, local, 0]
        if r < ROWS:
            return jnp.where(upper == 0, from_cross, from_chip).astype(jnp.int32)
        return jnp.where(upper == 0, from_chip, from_cross).astype(jnp.int32)

    def shifted(r, value):
        ring[r, :blocks, :] = value
        ring[r, blocks:, :] = value
        offset = shift_of(r)
        hops = offset // LANES
        rest = offset % LANES
        near = ring[r, pl.ds(blocks - hops, blocks), :]
        far = ring[r, pl.ds(blocks - 1 - hops, blocks), :]
        return pltpu.roll(jnp.where(lane < LANES - rest, near, far), rest, axis=1)

    margin = 0
    for step in range(STEPS):
        for r in range(margin + 2, 3 * ROWS - margin - 2):
            centre, change = tendency(state, r, speed[0, r], speed[1, r], lane)
            section[r] = inside(r, centre + change)
        if step == 0:
            for tail in tails:
                tail.wait()
        for r in range(margin + 4, 3 * ROWS - margin - 4):
            centre, change = tendency(section, r, speed[0, r], speed[1, r], lane)
            value = shifted(r, inside(r, 0.5 * (state[r] + centre + change)))
            if step + 1 < STEPS:
                state[r] = value
            else:
                out[pl.ds(r - ROWS, blocks, stride=ROWS), :] = value
        margin += 4


def in_vmem(value):
    return pltpu.with_memory_space_constraint(value, pltpu.VMEM)


def shards(fields, velocity, offsets):
    slabs = fields.shape[0] * fields.shape[1]
    blocks = lax.axis_size("az")
    count = lax.axis_size("rad")
    vmem = pl.BlockSpec(memory_space=pltpu.VMEM)
    smem = pl.BlockSpec(memory_space=pltpu.SMEM)

    sent = jnp.pad(fields.reshape(slabs, ROWS, LANES), ((0, blocks - slabs), (0, 0), (0, 0)))
    speeds = jnp.broadcast_to(velocity.reshape(1, 2 * ROWS, LANES), (blocks, 2 * ROWS, LANES))
    sent = jnp.concatenate([sent, speeds], axis=1)
    arrived = lax.all_to_all(sent, "az", 0, 0, tiled=True)
    size = 3 * ROWS * blocks + ROWS
    own = pl.pallas_call(
        gather_kernel,
        out_shape=pltpu.VMEM((size, LANES), jnp.float32),
        in_specs=[smem, vmem],
        out_specs=vmem,
        name="rows",
    )(offsets, in_vmem(arrived.reshape(blocks * 3 * ROWS, LANES)))

    def device(a, r):
        return a * count + r % count

    partner = [(device(a, r), device(a, r ^ 1)) for a in range(slabs) for r in range(count)]
    pairs = [[device(a, r), device(a, r + 1)] for a in range(slabs) for r in range(1, count, 2)]
    pairs += [[device(a, r), device(a, r + 1)] for a in range(slabs, blocks) for r in range(0, count, 2)]
    chip = lax.ppermute(own, ("az", "rad"), partner)
    cross = lax.all_gather(own, ("az", "rad"), axis_index_groups=pairs, tiled=True)

    done = pl.pallas_call(
        steps_kernel,
        out_shape=pltpu.VMEM((blocks * ROWS, LANES), jnp.float32),
        in_specs=[smem, vmem, vmem, vmem],
        out_specs=vmem,
        scratch_shapes=[
            pltpu.VMEM((3 * ROWS, blocks, LANES), jnp.float32),
            pltpu.VMEM((3 * ROWS, blocks, LANES), jnp.float32),
            pltpu.VMEM((3 * ROWS, 2 * blocks, LANES), jnp.float32),
            pltpu.VMEM((2, 3 * ROWS, blocks, LANES), jnp.float32),
            pltpu.SMEM((2, ROWS, LANES), jnp.float32),
            pltpu.SemaphoreType.DMA((2,)),
        ],
        name="disc_steps",
    )(offsets, in_vmem(own), in_vmem(chip), in_vmem(cross))
    back = lax.all_to_all(done.reshape(blocks, ROWS, LANES), "az", 0, 0, tiled=True)
    return back[:slabs].reshape(fields.shape)


def solution(mesh):
    placed = (P(None, None, "rad", "az"), P(None, "rad", "az"), P("rad"))
    return jax.shard_map(
        shards, mesh=mesh, in_specs=placed, out_specs=P(None, None, "rad", "az"), check_vma=False
    )
```

time: 67.1 us -> 57.2 us (0.85)
  the two profiles are of different devices: /device:TPU:40 before, /device:TPU:2 now
where the time goes in v2:
time: 57.2 us; the launch traced here: 56.9 us
  blocking collectives  50.5 us (88%)
  Pallas kernels  3.03 us (5%)
  starting transfers between devices  1.92 us (3%)
  local copies, waits for them, and re-layouts  1.41 us (2%)
    all_to_all x1, blocking collectives, shards(): arrived = lax.all_to_all(sent, 'az', 0, 0, tiled=True)  20.1 us
    all_gather x1, blocking collectives, shards(): lax.all_gather(own, ('az', 'rad'), axis_index_groups=pairs, tiled=True)  19.4 us
    all_to_all x1, blocking collectives, shards(): lax.all_to_all(done.reshape(blocks, ROWS, LANES), 'az', 0, 0, tiled=True)  11 us
    pallas_call x1, Pallas kernels, shards(): pl.pallas_call(steps_kernel, out_shape=pltpu.VMEM((blocks * ROWS, LANES),...  2.33 us
    ppermute x1, starting transfers between devices, shards(): chip = lax.ppermute(own, ('az', 'rad'), partner)  1.92 us
  transfers between devices with their start and end apart: 1, of which 0 were waited for; matrix products, arithmetic and copies ran while one was open for 0% of the time, Pallas kernels for 0%

profile of v2, /device:TPU:2, one launch (start us, length us, event | category | flops | bytes accessed | tf_op | source)
XLA Modules:
  0.0 56.9 jit_solution(18227312061977070730)
XLA Ops:
  0.0 0.0 copy-start
  0.0 0.7 %broadcast_in_dim.8 = f32[16,16,128]{2,1,0:T(8,128)S(1)} broadcast(f32[16,128]{1,0:T(8,128)} %bitcast.8), dimensions={1,2} | broadcast | bytes 139264 | tf_op jit(solution)/shard_map/broadcast_in_dim | solution.py:144
  0.7 0.1 copy-done
  0.8 20.1 %all_to_all.10 = f32[16,24,128]{2,1,0:T(8,128)S(1)} all-to-all(f32[16,24,128]{2,1,0:T(8,128)S(1)} %select_maximum_fusion), channel_id=1, replica_groups=mesh['az'=16,'rad'=48] {'az'}, dimensions={0} | all-to-all | bytes 393216 | tf_op jit(solution)/shard_map/all_to_all | solution.py:146
  20.9 0.7 %rows.1.own = f32[392,128]{1,0:T(8,128)S(1)} custom-call(s32[8]{0:T(128)} %offsets.3, f32[384,128]{1,0:T(8,128)S(1)} %bitcast.5), custom_call_target="tpu_custom_call" | custom-call | tf_op jit(solution)/shard_map/rows/pallas_call | solution.py:148
  21.6 1.9 %collective-permute-start = (f32[392,128]{1,0:T(8,128)S(1)}, f32[392,128]{1,0:T(8,128)S(1)}, u32[]{:S(2)}, u32[]{:S(2)}) collective-permute-start(f32[392,128]{1,0:T(8,128)S(1)} %rows.1.own), channel_id=1, source_target_pairs={{0,1},{1,0},{2,3},{3,2},{4,5},{5,4},{6,7},{7,6},{8,9},{9,8},{10,11... | collective-permute-start | bytes 602120 | tf_op jit(solution)/shard_map/ppermute | solution.py:162
  23.6 19.4 %all_gather.3.cross = f32[784,128]{1,0:T(8,128)S(1)} all-gather(f32[392,128]{1,0:T(8,128)S(1)} %rows.1.own), channel_id=1, replica_groups={{1,2},{3,4},{5,6},{7,8},{9,10},{11,12},{13,14},{15,16},{17,18},{19,20},..., dimensions={0}, use_global_device_ids=true | all-gather | bytes 602112 | tf_op jit(solution)/shard_map/all_gather | solution.py:163
  42.9 0.0 collective-permute-done.chip
  42.9 2.3 %disc_steps.1 = f32[128,128]{1,0:T(8,128)S(1)} custom-call(s32[8]{0:T(128)} %offsets.3, f32[392,128]{1,0:T(8,128)S(1)} %rows.1.own, f32[392,128]{1,0:T(8,128)S(1)} %collective-permute-done.chip, f32[784,128]{1,0:T(8,128)S(1)} %all_gather.3.cross), custom_call_target="tpu_custom_call" | custom-call | tf_op jit(solution)/shard_map/disc_steps/pallas_call | solution.py:165
  45.3 11.0 %all_to_all.11 = f32[16,8,128]{2,1,0:T(8,128)S(1)} all-to-all(f32[16,8,128]{2,1,0:T(8,128)S(1)} %bitcast.6), channel_id=1, replica_groups=mesh['az'=16,'rad'=48] {'az'}, dimensions={0} | all-to-all | bytes 131072 | tf_op jit(solution)/shard_map/all_to_all | solution.py:180
  56.3 0.6 %slice.4 = f32[10,8,128]{2,1,0:T(8,128)} slice(f32[16,8,128]{2,1,0:T(8,128)S(1)} %all_to_all.11), slice={[0:10], [0:8], [0:128]} | slice | bytes 81920 | tf_op jit(solution)/shard_map/slice | solution.py:181
  (1 shorter events, 0.0 us)
Async XLA Ops:
  0.0 0.8 %copy-start = (f32[5,2,8,128]{3,2,1,0:T(8,128)S(1)}, f32[5,2,8,128]{3,2,1,0:T(8,128)}, u32[]{:S(2)}) copy-start(f32[5,2,8,128]{3,2,1,0:T(8,128)} %param.3) | copy-start | bytes 122884
  21.6 21.3 %collective-permute-start = (f32[392,128]{1,0:T(8,128)S(1)}, f32[392,128]{1,0:T(8,128)S(1)}, u32[]{:S(2)}, u32[]{:S(2)}) collective-permute-start(f32[392,128]{1,0:T(8,128)S(1)} %rows.1.own), channel_id=1, source_target_pairs={{0,1},{1,0},{2,3},{3,2},{4,5},{5,4},{6,7},{7,6},{8,9},{9,8},{10,11... | collective-permute-start | bytes 602120 | tf_op jit(solution)/shard_map/ppermute | solution.py:162

commit v3 on v2

v3 whole, which is shorter than its diff:
```python
import jax
import jax.numpy as jnp
from jax import lax
from jax.experimental import pallas as pl
from jax.experimental.pallas import tpu as pltpu
from jax.sharding import PartitionSpec as P

STEPS = 2
VISCOSITY = 0.05
LANES = 128
ROWS = 8
HALO = 4
PARTS = 4


def around(row, lane):
    blocks = row.shape[0]
    behind = pltpu.roll(row, 1, axis=0)
    ahead = pltpu.roll(row, blocks - 1, axis=0)
    m2 = pltpu.roll(jnp.where(lane >= LANES - 2, behind, row), 2, axis=1)
    m1 = pltpu.roll(jnp.where(lane >= LANES - 1, behind, row), 1, axis=1)
    p1 = pltpu.roll(jnp.where(lane < 1, ahead, row), LANES - 1, axis=1)
    p2 = pltpu.roll(jnp.where(lane < 2, ahead, row), LANES - 2, axis=1)
    return m2, m1, p1, p2


def tendency(field, r, v_r, v_p, lane):
    centre = field[r]
    m2, m1, p1, p2 = around(centre, lane)
    r_m2, r_m1, r_p1, r_p2 = field[r - 2], field[r - 1], field[r + 1], field[r + 2]
    near = (m1 + p1) + (r_m1 + r_p1)
    far = (m2 + p2) + (r_m2 + r_p2)
    slope_p = (p1 - m1) * (8.0 / 12.0) - (p2 - m2) * (1.0 / 12.0)
    slope_r = (r_p1 - r_m1) * (8.0 / 12.0) - (r_p2 - r_m2) * (1.0 / 12.0)
    scale = VISCOSITY / 12.0
    curve = near * (16.0 * scale) - far * scale - centre * (60.0 * scale)
    return centre, curve - v_p * slope_p - v_r * slope_r


def row_of(arrived, part, r):
    blocks = arrived.shape[0] // (3 * ROWS)
    return arrived[pl.ds(part * ROWS + r, blocks, stride=3 * ROWS), :]


def send_kernel(fields, velocity, offsets, sent, noted):
    slabs = fields.shape[0] // ROWS
    for k in range(sent.shape[0] // (3 * ROWS)):
        at = k * 3 * ROWS
        if k < slabs:
            sent[pl.ds(at, ROWS), :] = fields[pl.ds(k * ROWS, ROWS), :]
        else:
            sent[pl.ds(at, ROWS), :] = jnp.zeros((ROWS, LANES), jnp.float32)
        sent[pl.ds(at + ROWS, 2 * ROWS), :] = velocity[...]
    noted[...] = jnp.zeros((ROWS, LANES), jnp.float32)
    noted[:1, :ROWS] = offsets[...].astype(jnp.float32)


def show_kernel(noted, arrived, to_chip, to_cross):
    blocks = arrived.shape[0] // (3 * ROWS)
    lane = lax.broadcasted_iota(jnp.int32, (blocks, LANES), 1)
    first = lax.axis_index("rad") % 2 == 0
    slab = [row_of(arrived, 0, r) for r in range(ROWS)]
    speed = [[row_of(arrived, 1 + c, r) for r in range(ROWS)] for c in range(2)]

    def put(ref, part, k, value):
        ref[pl.ds((part * HALO + k) * blocks, blocks), :] = value

    for k in range(HALO):
        r = 2 + k
        centre, change = tendency(slab, r, speed[0][r], speed[1][r], lane)
        put(to_chip, 1, k, centre + change)
        put(to_cross, 1, k, centre + change)
        for part, rows in ((0, slab), (2, speed[0]), (3, speed[1])):
            near_low, near_high = rows[k], rows[ROWS - HALO + k]
            put(to_chip, part, k, jnp.where(first, near_high, near_low))
            put(to_cross, part, k, jnp.where(first, near_low, near_high))
    for ref in (to_chip, to_cross):
        ref[pl.ds(PARTS * HALO * blocks, ROWS), :] = noted[...]


def steps_kernel(arrived, shown, chip, cross, out, state, section, ring, speed, shifts, sem):
    size = shown.shape[0]
    blocks = arrived.shape[0] // (3 * ROWS)
    lane = lax.broadcasted_iota(jnp.int32, (blocks, LANES), 1)
    place = lax.axis_index("rad")
    upper = place % 2
    first = upper == 0
    chip_at = (1 - upper) * size if chip.shape[0] > size else 0
    cross_at = upper * size
    tails = [
        pltpu.make_async_copy(ref.at[pl.ds(at + size - ROWS, ROWS)], shifts.at[i], sem.at[i])
        for i, (ref, at) in enumerate(((shown, 0), (chip, chip_at), (cross, cross_at)))
    ]
    for tail in tails:
        tail.start()
    has_low = place > 0
    has_high = place < lax.axis_size("rad") - 1

    def inside(r, value):
        if r < ROWS:
            return jnp.where(has_low, value, 0.0)
        if r >= 2 * ROWS:
            return jnp.where(has_high, value, 0.0)
        return value

    for r in range(ROWS):
        state[ROWS + r] = row_of(arrived, 0, r)
        for c in range(2):
            speed[c, ROWS + r] = row_of(arrived, 1 + c, r)
    for k in range(HALO):
        section[ROWS + 2 + k] = shown[pl.ds((HALO + k) * blocks, blocks), :]
        for part in range(PARTS):
            start = (part * HALO + k) * blocks
            from_chip = chip[pl.ds(chip_at + start, blocks), :]
            from_cross = cross[pl.ds(cross_at + start, blocks), :]
            low = jnp.where(first, from_cross, from_chip)
            high = jnp.where(first, from_chip, from_cross)
            below, above = ROWS - HALO + k, 2 * ROWS + k
            if part == 0:
                state[below] = inside(below, low)
                state[above] = inside(above, high)
            elif part == 1:
                section[2 + k] = inside(2 + k, low)
                section[2 * ROWS + 2 + k] = inside(2 * ROWS + 2 + k, high)
            else:
                speed[part - 2, below] = low
                speed[part - 2, above] = high

    def shift_of(r):
        local = r % ROWS
        if r // ROWS == 1:
            return shifts[0, 0, local].astype(jnp.int32)
        from_chip = shifts[1, 0, local]
        from_cross = shifts[2, 0, local]
        if r < ROWS:
            return jnp.where(first, from_cross, from_chip).astype(jnp.int32)
        return jnp.where(first, from_chip, from_cross).astype(jnp.int32)

    def shifted(r, value):
        ring[r, :blocks, :] = value
        ring[r, blocks:, :] = value
        offset = shift_of(r)
        hops = offset // LANES
        rest = offset % LANES
        near = ring[r, pl.ds(blocks - hops, blocks), :]
        far = ring[r, pl.ds(blocks - 1 - hops, blocks), :]
        return pltpu.roll(jnp.where(lane < LANES - rest, near, far), rest, axis=1)

    margin = 0
    for step in range(STEPS):
        for r in range(margin + 2, 3 * ROWS - margin - 2):
            if step > 0 or not 2 <= r % ROWS < 2 + HALO:
                centre, change = tendency(state, r, speed[0, r], speed[1, r], lane)
                section[r] = inside(r, centre + change)
        if step == 0:
            for tail in tails:
                tail.wait()
        for r in range(margin + 4, 3 * ROWS - margin - 4):
            centre, change = tendency(section, r, speed[0, r], speed[1, r], lane)
            value = shifted(r, inside(r, 0.5 * (state[r] + centre + change)))
            if step + 1 < STEPS:
                state[r] = value
            else:
                out[pl.ds(r - ROWS, blocks, stride=ROWS), :] = value
        margin += 4


def in_vmem(value):
    return pltpu.with_memory_space_constraint(value, pltpu.VMEM)


def shards(fields, velocity, offsets):
    slabs = fields.shape[0] * fields.shape[1]
    blocks = lax.axis_size("az")
    count = lax.axis_size("rad")
    vmem = pl.BlockSpec(memory_space=pltpu.VMEM)

    sent, noted = pl.pallas_call(
        send_kernel,
        out_shape=[
            pltpu.VMEM((blocks * 3 * ROWS, LANES), jnp.float32),
            pltpu.VMEM((ROWS, LANES), jnp.float32),
        ],
        in_specs=[vmem] * 3,
        out_specs=[vmem] * 2,
        name="send",
    )(
        fields.reshape(slabs * ROWS, LANES),
        velocity.reshape(2 * ROWS, LANES),
        offsets.reshape(1, ROWS),
    )
    arrived = lax.all_to_all(sent.reshape(blocks, 3 * ROWS, LANES), "az", 0, 0, tiled=True)
    arrived = in_vmem(arrived.reshape(blocks * 3 * ROWS, LANES))
    size = PARTS * HALO * blocks + ROWS
    to_chip, to_cross = pl.pallas_call(
        show_kernel,
        out_shape=[pltpu.VMEM((size, LANES), jnp.float32)] * 2,
        in_specs=[vmem, vmem],
        out_specs=[vmem, vmem],
        name="show",
    )(in_vmem(noted), arrived)

    def device(a, r):
        return a * count + r % count

    pairs = [[device(a, r), device(a, r + 1)] for a in range(slabs) for r in range(1, count, 2)]
    pairs += [[device(a, r), device(a, r + 1)] for a in range(slabs, blocks) for r in range(0, count, 2)]
    twins = [[r, r + 1] for r in range(0, count, 2)]
    chip = lax.all_gather(to_chip, "rad", axis_index_groups=twins, tiled=True)
    cross = lax.all_gather(to_cross, ("az", "rad"), axis_index_groups=pairs, tiled=True)

    done = pl.pallas_call(
        steps_kernel,
        out_shape=pltpu.VMEM((blocks * ROWS, LANES), jnp.float32),
        in_specs=[vmem] * 4,
        out_specs=vmem,
        scratch_shapes=[
            pltpu.VMEM((3 * ROWS, blocks, LANES), jnp.float32),
            pltpu.VMEM((3 * ROWS, blocks, LANES), jnp.float32),
            pltpu.VMEM((3 * ROWS, 2 * blocks, LANES), jnp.float32),
            pltpu.VMEM((2, 3 * ROWS, blocks, LANES), jnp.float32),
            pltpu.SMEM((3, ROWS, LANES), jnp.float32),
            pltpu.SemaphoreType.DMA((3,)),
        ],
        name="disc_steps",
    )(arrived, in_vmem(to_cross), in_vmem(chip), in_vmem(cross))
    back = lax.all_to_all(done.reshape(blocks, ROWS, LANES), "az", 0, 0, tiled=True)
    return back[:slabs].reshape(fields.shape)


def solution(mesh):
    placed = (P(None, None, "rad", "az"), P(None, "rad", "az"), P("rad"))
    return jax.shard_map(
        shards, mesh=mesh, in_specs=placed, out_specs=P(None, None, "rad", "az"), check_vma=False
    )
```

time: 57.2 us -> 53.3 us (0.932)
  starting transfers between devices: 1.92 us -> 0 us
  local copies, waits for them, and re-layouts: 1.41 us -> 0.62 us
  blocking collectives: 50.5 us -> 49.8 us
    ppermute x1 -> x0, starting transfers between devices: 1.92 us -> none  [shards(): chip = lax.ppermute(own, ('az', 'rad'), partner)]
    all_gather x1 -> x2, blocking collectives: 19.4 us -> 18.3 us  [the longest x1 16.3 us: shards(): lax.all_gather(to_cross, ('az', 'rad'), axis_index_groups=pairs, tiled=True)]
    broadcast_in_dim x1 -> x0, local copies, waits for them, and re-layouts: 0.71 us -> none  [shards(): jnp.broadcast_to(velocity.reshape(1, 2 * ROWS, LANES), (blocks, 2 * ROWS,...]
    pallas_call x1, Pallas kernels: 2.33 us -> 1.72 us  [shards(): pl.pallas_call(steps_kernel, out_shape=pltpu.VMEM((blocks * ROWS, LANES),...]
  transfers between devices with their start and end apart: 1 -> 0, of which waited for: 0 -> 0; matrix products, arithmetic and copies ran while one was open for 0% -> 0% of each run, Pallas kernels for 0% -> 0%
where the time goes in v3:
time: 53.3 us; the launch traced here: 53 us
  blocking collectives  49.8 us (93%)
  Pallas kernels  2.64 us (5%)
  local copies, waits for them, and re-layouts  0.62 us (1%)
    all_to_all x1, blocking collectives, shards(): lax.all_to_all(sent.reshape(blocks, 3 * ROWS, LANES), 'az', 0, 0, tiled=T...  20.1 us
    all_gather x1, blocking collectives, shards(): lax.all_gather(to_cross, ('az', 'rad'), axis_index_groups=pairs, tiled=True)  16.3 us
    all_to_all x1, blocking collectives, shards(): lax.all_to_all(done.reshape(blocks, ROWS, LANES), 'az', 0, 0, tiled=True)  11.3 us
    all_gather x1, blocking collectives, shards(): chip = lax.all_gather(to_chip, 'rad', axis_index_groups=twins, tiled=True)  2 us
    pallas_call x1, Pallas kernels, shards(): pl.pallas_call(steps_kernel, out_shape=pltpu.VMEM((blocks * ROWS, LANES),...  1.72 us

profile of v3, /device:TPU:2, one launch (start us, length us, event | category | flops | bytes accessed | tf_op | source)
XLA Modules:
  0.0 53.0 jit_solution(10298488391768186878)
XLA Ops:
  0.0 0.8 %send.1 = (f32[384,128]{1,0:T(8,128)S(1)}, f32[8,128]{1,0:T(8,128)S(1)}) custom-call(f32[80,128]{1,0:T(8,128)} %bitcast.11, f32[16,128]{1,0:T(8,128)} %bitcast.12, s32[1,8]{1,0:T(1,128)} %bitcast.13), custom_call_target="tpu_custom_call" | custom-call | tf_op jit(solution)/shard_map/send/pallas_call | solution.py:178
  0.8 20.1 %all_to_all.10 = f32[16,24,128]{2,1,0:T(8,128)S(1)} all-to-all(f32[16,24,128]{2,1,0:T(8,128)S(1)} %bitcast.10), channel_id=1, replica_groups=mesh['az'=16,'rad'=48] {'az'}, dimensions={0} | all-to-all | bytes 393216 | tf_op jit(solution)/shard_map/all_to_all | solution.py:192
  20.9 0.1 show.1
  21.0 2.0 %all_gather.6.chip = f32[528,128]{1,0:T(8,128)S(1)} all-gather(f32[264,128]{1,0:T(8,128)S(1)} %get-tuple-element.12), channel_id=1, replica_groups={{0,1},{2,3},{4,5},{6,7},{8,9},{10,11},{12,13},{14,15},{16,17},{18,19},{..., dimensions={0}, use_global_device_ids=true | all-gather | bytes 405504 | tf_op jit(solution)/shard_map/all_gather | solution.py:209
  23.0 16.3 %all_gather.7.cross = f32[528,128]{1,0:T(8,128)S(1)} all-gather(f32[264,128]{1,0:T(8,128)S(1)} %get-tuple-element.11.shown), channel_id=1, replica_groups={{1,2},{3,4},{5,6},{7,8},{9,10},{11,12},{13,14},{15,16},{17,18},{19,20},..., dimensions={0}, use_global_device_ids=true | all-gather | bytes 405504 | tf_op jit(solution)/shard_map/all_gather | solution.py:210
  39.4 1.7 %disc_steps.1 = f32[128,128]{1,0:T(8,128)S(1)} custom-call(f32[384,128]{1,0:T(8,128)S(1)} %bitcast.8, f32[264,128]{1,0:T(8,128)S(1)} %get-tuple-element.11.shown, f32[528,128]{1,0:T(8,128)S(1)} %all_gather.6.chip, f32[528,128]{1,0:T(8,128)S(1)} %all_gather.7.cross), custom_call_target="tpu_custom_call" | custom-call | tf_op jit(solution)/shard_map/disc_steps/pallas_call | solution.py:212
  41.1 11.3 %all_to_all.11 = f32[16,8,128]{2,1,0:T(8,128)S(1)} all-to-all(f32[16,8,128]{2,1,0:T(8,128)S(1)} %bitcast.9), channel_id=1, replica_groups=mesh['az'=16,'rad'=48] {'az'}, dimensions={0} | all-to-all | bytes 131072 | tf_op jit(solution)/shard_map/all_to_all | solution.py:227
  52.4 0.6 %slice.4 = f32[10,8,128]{2,1,0:T(8,128)} slice(f32[16,8,128]{2,1,0:T(8,128)S(1)} %all_to_all.11), slice={[0:10], [0:8], [0:128]} | slice | bytes 81920 | tf_op jit(solution)/shard_map/slice | solution.py:228

commit v4 on v3

--- a/solution.py
+++ b/solution.py
@@ -86,7 +86,7 @@
     upper = place % 2
     first = upper == 0
     chip_at = (1 - upper) * size if chip.shape[0] > size else 0
-    cross_at = upper * size
+    cross_at = upper * size if cross.shape[0] > size else 0
     tails = [
         pltpu.make_async_copy(ref.at[pl.ds(at + size - ROWS, ROWS)], shifts.at[i], sem.at[i])
         for i, (ref, at) in enumerate(((shown, 0), (chip, chip_at), (cross, cross_at)))
@@ -203,11 +203,11 @@
     def device(a, r):
         return a * count + r % count
 
-    pairs = [[device(a, r), device(a, r + 1)] for a in range(slabs) for r in range(1, count, 2)]
-    pairs += [[device(a, r), device(a, r + 1)] for a in range(slabs, blocks) for r in range(0, count, 2)]
+    swaps = [(device(a, r), device(a, r + 1)) for a in range(slabs) for r in range(1, count - 1, 2)]
+    swaps += [(high, low) for low, high in swaps]
     twins = [[r, r + 1] for r in range(0, count, 2)]
     chip = lax.all_gather(to_chip, "rad", axis_index_groups=twins, tiled=True)
-    cross = lax.all_gather(to_cross, ("az", "rad"), axis_index_groups=pairs, tiled=True)
+    cross = lax.ppermute(to_cross, ("az", "rad"), swaps)
 
     done = pl.pallas_call(
         steps_kernel,

time: 53.3 us -> 49.7 us (0.932)
  the two profiles are of different devices: /device:TPU:2 before, /device:TPU:1 now
where the time goes in v4:
time: 49.7 us; the launch traced here: 49.4 us
  blocking collectives  30.3 us (61%)
  starting transfers between devices  12.5 us (25%)
  waiting for transfers between devices  3.3 us (7%)
  Pallas kernels  2.65 us (5%)
  local copies, waits for them, and re-layouts  0.62 us (1%)
    all_to_all x1, blocking collectives, shards(): lax.all_to_all(sent.reshape(blocks, 3 * ROWS, LANES), 'az', 0, 0, tiled=T...  18.5 us
    ppermute x1, starting transfers between devices, shards(): cross = lax.ppermute(to_cross, ('az', 'rad'), swaps)  12.5 us
    all_to_all x1, blocking collectives, shards(): lax.all_to_all(done.reshape(blocks, ROWS, LANES), 'az', 0, 0, tiled=True)  9.83 us
    ppermute x1, waiting for transfers between devices, shards(): cross = lax.ppermute(to_cross, ('az', 'rad'), swaps)  3.3 us
    all_gather x1, blocking collectives, shards(): chip = lax.all_gather(to_chip, 'rad', axis_index_groups=twins, tiled=True)  2 us
    pallas_call x1, Pallas kernels, shards(): pl.pallas_call(steps_kernel, out_shape=pltpu.VMEM((blocks * ROWS, LANES),...  1.72 us
  transfers between devices with their start and end apart: 1, of which 1 were waited for; matrix products, arithmetic and copies ran while one was open for 0% of the time, Pallas kernels for 0%

profile of v4, /device:TPU:1, one launch (start us, length us, event | category | flops | bytes accessed | tf_op | source)
XLA Modules:
  0.0 49.4 jit_solution(7368365278947453037)
XLA Ops:
  0.0 0.8 %send.1 = (f32[384,128]{1,0:T(8,128)S(1)}, f32[8,128]{1,0:T(8,128)S(1)}) custom-call(f32[80,128]{1,0:T(8,128)} %bitcast.11, f32[16,128]{1,0:T(8,128)} %bitcast.12, s32[1,8]{1,0:T(1,128)} %bitcast.13), custom_call_target="tpu_custom_call" | custom-call | tf_op jit(solution)/shard_map/send/pallas_call | solution.py:178
  0.8 18.5 %all_to_all.10 = f32[16,24,128]{2,1,0:T(8,128)S(1)} all-to-all(f32[16,24,128]{2,1,0:T(8,128)S(1)} %bitcast.10), channel_id=1, replica_groups=mesh['az'=16,'rad'=48] {'az'}, dimensions={0} | all-to-all | bytes 393216 | tf_op jit(solution)/shard_map/all_to_all | solution.py:192
  19.3 0.1 show.1
  19.4 12.5 %collective-permute-start = (f32[264,128]{1,0:T(8,128)S(1)}, f32[264,128]{1,0:T(8,128)S(1)}, u32[]{:S(2)}, u32[]{:S(2)}) collective-permute-start(f32[264,128]{1,0:T(8,128)S(1)} %get-tuple-element.11.shown), channel_id=1, source_target_pairs={{1,2},{3,4},{5,6},{7,8},{9,10},{11,12},{13,14},{15,16},{17,18},{19... | collective-permute-start | bytes 405512 | tf_op jit(solution)/shard_map/ppermute | solution.py:210
  31.9 2.0 %all_gather.3.chip = f32[528,128]{1,0:T(8,128)S(1)} all-gather(f32[264,128]{1,0:T(8,128)S(1)} %get-tuple-element.12), channel_id=1, replica_groups={{0,1},{2,3},{4,5},{6,7},{8,9},{10,11},{12,13},{14,15},{16,17},{18,19},{..., dimensions={0}, use_global_device_ids=true | all-gather | bytes 405504 | tf_op jit(solution)/shard_map/all_gather | solution.py:209
  33.9 3.3 %collective-permute-done.cross = f32[264,128]{1,0:T(8,128)S(1)} collective-permute-done((f32[264,128]{1,0:T(8,128)S(1)}, f32[264,128]{1,0:T(8,128)S(1)}, u32[]{:S(2)}, u32[]{:S(2)}) %collective-permute-start) | collective-permute-done | bytes 135200 | tf_op jit(solution)/shard_map/ppermute | solution.py:210
  37.2 1.7 %disc_steps.1 = f32[128,128]{1,0:T(8,128)S(1)} custom-call(f32[384,128]{1,0:T(8,128)S(1)} %bitcast.8, f32[264,128]{1,0:T(8,128)S(1)} %get-tuple-element.11.shown, f32[528,128]{1,0:T(8,128)S(1)} %all_gather.3.chip, f32[264,128]{1,0:T(8,128)S(1)} %collective-permute-done.cross), custom_call_target="tpu_custom_call" | custom-call | tf_op jit(solution)/shard_map/disc_steps/pallas_call | solution.py:212
  38.9 9.8 %all_to_all.11 = f32[16,8,128]{2,1,0:T(8,128)S(1)} all-to-all(f32[16,8,128]{2,1,0:T(8,128)S(1)} %bitcast.9), channel_id=1, replica_groups=mesh['az'=16,'rad'=48] {'az'}, dimensions={0} | all-to-all | bytes 131072 | tf_op jit(solution)/shard_map/all_to_all | solution.py:227
  48.8 0.6 %slice.4 = f32[10,8,128]{2,1,0:T(8,128)} slice(f32[16,8,128]{2,1,0:T(8,128)S(1)} %all_to_all.11), slice={[0:10], [0:8], [0:128]} | slice | bytes 81920 | tf_op jit(solution)/shard_map/slice | solution.py:228
Async XLA Ops:
  19.4 17.8 %collective-permute-start = (f32[264,128]{1,0:T(8,128)S(1)}, f32[264,128]{1,0:T(8,128)S(1)}, u32[]{:S(2)}, u32[]{:S(2)}) collective-permute-start(f32[264,128]{1,0:T(8,128)S(1)} %get-tuple-element.11.shown), channel_id=1, source_target_pairs={{1,2},{3,4},{5,6},{7,8},{9,10},{11,12},{13,14},{15,16},{17,18},{19... | collective-permute-start | bytes 405512 | tf_op jit(solution)/shard_map/ppermute | solution.py:210

commit v5 on v4

--- a/solution.py
+++ b/solution.py
@@ -30,10 +30,9 @@
     r_m2, r_m1, r_p1, r_p2 = field[r - 2], field[r - 1], field[r + 1], field[r + 2]
     near = (m1 + p1) + (r_m1 + r_p1)
     far = (m2 + p2) + (r_m2 + r_p2)
-    slope_p = (p1 - m1) * (8.0 / 12.0) - (p2 - m2) * (1.0 / 12.0)
-    slope_r = (r_p1 - r_m1) * (8.0 / 12.0) - (r_p2 - r_m2) * (1.0 / 12.0)
-    scale = VISCOSITY / 12.0
-    curve = near * (16.0 * scale) - far * scale - centre * (60.0 * scale)
+    slope_p = (p1 - m1) * 8.0 - (p2 - m2)
+    slope_r = (r_p1 - r_m1) * 8.0 - (r_p2 - r_m2)
+    curve = (near * 16.0 - far - centre * 60.0) * (VISCOSITY / 12.0)
     return centre, curve - v_p * slope_p - v_r * slope_r
 
 
@@ -44,13 +43,15 @@
 
 def send_kernel(fields, velocity, offsets, sent, noted):
     slabs = fields.shape[0] // ROWS
-    for k in range(sent.shape[0] // (3 * ROWS)):
+    blocks = sent.shape[0] // (3 * ROWS)
+    speed = velocity[...] * (1.0 / 12.0)
+    for k in range(blocks):
         at = k * 3 * ROWS
         if k < slabs:
             sent[pl.ds(at, ROWS), :] = fields[pl.ds(k * ROWS, ROWS), :]
         else:
             sent[pl.ds(at, ROWS), :] = jnp.zeros((ROWS, LANES), jnp.float32)
-        sent[pl.ds(at + ROWS, 2 * ROWS), :] = velocity[...]
+        sent[pl.ds(at + ROWS, 2 * ROWS), :] = speed
     noted[...] = jnp.zeros((ROWS, LANES), jnp.float32)
     noted[:1, :ROWS] = offsets[...].astype(jnp.float32)
 
@@ -136,9 +137,7 @@
             return jnp.where(first, from_cross, from_chip).astype(jnp.int32)
         return jnp.where(first, from_chip, from_cross).astype(jnp.int32)
 
-    def shifted(r, value):
-        ring[r, :blocks, :] = value
-        ring[r, blocks:, :] = value
+    def shifted(r):
         offset = shift_of(r)
         hops = offset // LANES
         rest = offset % LANES
@@ -152,16 +151,20 @@
             if step > 0 or not 2 <= r % ROWS < 2 + HALO:
                 centre, change = tendency(state, r, speed[0, r], speed[1, r], lane)
                 section[r] = inside(r, centre + change)
+        inner = range(margin + 4, 3 * ROWS - margin - 4)
+        for r in inner:
+            centre, change = tendency(section, r, speed[0, r], speed[1, r], lane)
+            value = inside(r, 0.5 * (state[r] + centre + change))
+            ring[r, :blocks, :] = value
+            ring[r, blocks:, :] = value
         if step == 0:
             for tail in tails:
                 tail.wait()
-        for r in range(margin + 4, 3 * ROWS - margin - 4):
-            centre, change = tendency(section, r, speed[0, r], speed[1, r], lane)
-            value = shifted(r, inside(r, 0.5 * (state[r] + centre + change)))
+        for r in inner:
             if step + 1 < STEPS:
-                state[r] = value
+                state[r] = shifted(r)
             else:
-                out[pl.ds(r - ROWS, blocks, stride=ROWS), :] = value
+                out[pl.ds(r - ROWS, blocks, stride=ROWS), :] = shifted(r)
         margin += 4
 
 

time: 49.7 us -> 49.3 us (level)
  no operation moved by 1% of the time
where the time goes in v5:
time: 49.3 us; the launch traced here: 49 us
  blocking collectives  30.3 us (61%)
  starting transfers between devices  12.5 us (25%)
  waiting for transfers between devices  3.3 us (7%)
  Pallas kernels  2.19 us (4%)
  local copies, waits for them, and re-layouts  0.62 us (1%)
    all_to_all x1, blocking collectives, shards(): lax.all_to_all(sent.reshape(blocks, 3 * ROWS, LANES), 'az', 0, 0, tiled=T...  18.5 us
    ppermute x1, starting transfers between devices, shards(): cross = lax.ppermute(to_cross, ('az', 'rad'), swaps)  12.5 us
    all_to_all x1, blocking collectives, shards(): lax.all_to_all(done.reshape(blocks, ROWS, LANES), 'az', 0, 0, tiled=True)  9.83 us
    ppermute x1, waiting for transfers between devices, shards(): cross = lax.ppermute(to_cross, ('az', 'rad'), swaps)  3.3 us
    all_gather x1, blocking collectives, shards(): chip = lax.all_gather(to_chip, 'rad', axis_index_groups=twins, tiled=True)  2 us
    pallas_call x1, Pallas kernels, shards(): pl.pallas_call(steps_kernel, out_shape=pltpu.VMEM((blocks * ROWS, LANES),...  1.27 us
  transfers between devices with their start and end apart: 1, of which 1 were waited for; matrix products, arithmetic and copies ran while one was open for 0% of the time, Pallas kernels for 0%

profile of v5, /device:TPU:1, one launch (start us, length us, event | category | flops | bytes accessed | tf_op | source)
XLA Modules:
  0.0 49.0 jit_solution(3732581237690728781)
XLA Ops:
  0.0 0.8 %send.1 = (f32[384,128]{1,0:T(8,128)S(1)}, f32[8,128]{1,0:T(8,128)S(1)}) custom-call(f32[80,128]{1,0:T(8,128)} %bitcast.11, f32[16,128]{1,0:T(8,128)} %bitcast.12, s32[1,8]{1,0:T(1,128)} %bitcast.13), custom_call_target="tpu_custom_call" | custom-call | tf_op jit(solution)/shard_map/send/pallas_call | solution.py:181
  0.8 18.5 %all_to_all.10 = f32[16,24,128]{2,1,0:T(8,128)S(1)} all-to-all(f32[16,24,128]{2,1,0:T(8,128)S(1)} %bitcast.10), channel_id=1, replica_groups=mesh['az'=16,'rad'=48] {'az'}, dimensions={0} | all-to-all | bytes 393216 | tf_op jit(solution)/shard_map/all_to_all | solution.py:195
  19.3 0.1 show.1
  19.4 12.5 %collective-permute-start = (f32[264,128]{1,0:T(8,128)S(1)}, f32[264,128]{1,0:T(8,128)S(1)}, u32[]{:S(2)}, u32[]{:S(2)}) collective-permute-start(f32[264,128]{1,0:T(8,128)S(1)} %get-tuple-element.11.shown), channel_id=1, source_target_pairs={{1,2},{3,4},{5,6},{7,8},{9,10},{11,12},{13,14},{15,16},{17,18},{19... | collective-permute-start | bytes 405512 | tf_op jit(solution)/shard_map/ppermute | solution.py:213
  31.9 2.0 %all_gather.3.chip = f32[528,128]{1,0:T(8,128)S(1)} all-gather(f32[264,128]{1,0:T(8,128)S(1)} %get-tuple-element.12), channel_id=1, replica_groups={{0,1},{2,3},{4,5},{6,7},{8,9},{10,11},{12,13},{14,15},{16,17},{18,19},{..., dimensions={0}, use_global_device_ids=true | all-gather | bytes 405504 | tf_op jit(solution)/shard_map/all_gather | solution.py:212
  33.9 3.3 %collective-permute-done.cross = f32[264,128]{1,0:T(8,128)S(1)} collective-permute-done((f32[264,128]{1,0:T(8,128)S(1)}, f32[264,128]{1,0:T(8,128)S(1)}, u32[]{:S(2)}, u32[]{:S(2)}) %collective-permute-start) | collective-permute-done | bytes 135200 | tf_op jit(solution)/shard_map/ppermute | solution.py:213
  37.2 1.3 %disc_steps.1 = f32[128,128]{1,0:T(8,128)S(1)} custom-call(f32[384,128]{1,0:T(8,128)S(1)} %bitcast.8, f32[264,128]{1,0:T(8,128)S(1)} %get-tuple-element.11.shown, f32[528,128]{1,0:T(8,128)S(1)} %all_gather.3.chip, f32[264,128]{1,0:T(8,128)S(1)} %collective-permute-done.cross), custom_call_target="tpu_custom_call" | custom-call | tf_op jit(solution)/shard_map/disc_steps/pallas_call | solution.py:215
  38.5 9.8 %all_to_all.11 = f32[16,8,128]{2,1,0:T(8,128)S(1)} all-to-all(f32[16,8,128]{2,1,0:T(8,128)S(1)} %bitcast.9), channel_id=1, replica_groups=mesh['az'=16,'rad'=48] {'az'}, dimensions={0} | all-to-all | bytes 131072 | tf_op jit(solution)/shard_map/all_to_all | solution.py:230
  48.3 0.6 %slice.4 = f32[10,8,128]{2,1,0:T(8,128)} slice(f32[16,8,128]{2,1,0:T(8,128)S(1)} %all_to_all.11), slice={[0:10], [0:8], [0:128]} | slice | bytes 81920 | tf_op jit(solution)/shard_map/slice | solution.py:231
Async XLA Ops:
  19.4 17.8 %collective-permute-start = (f32[264,128]{1,0:T(8,128)S(1)}, f32[264,128]{1,0:T(8,128)S(1)}, u32[]{:S(2)}, u32[]{:S(2)}) collective-permute-start(f32[264,128]{1,0:T(8,128)S(1)} %get-tuple-element.11.shown), channel_id=1, source_target_pairs={{1,2},{3,4},{5,6},{7,8},{9,10},{11,12},{13,14},{15,16},{17,18},{19... | collective-permute-start | bytes 405512 | tf_op jit(solution)/shard_map/ppermute | solution.py:213

commit v6 on v5

v6 whole, which is shorter than its diff:
```python
import jax
import jax.numpy as jnp
from jax import lax
from jax.experimental import pallas as pl
from jax.experimental.pallas import tpu as pltpu
from jax.sharding import PartitionSpec as P

VISCOSITY = 0.05
SCALE = VISCOSITY / 12.0
LANES = 128
ROWS = 8
SHOWN = (2, 2, 4, 4, 2)


def around(row, lane):
    blocks = row.shape[0]
    behind = pltpu.roll(row, 1, axis=0)
    ahead = pltpu.roll(row, blocks - 1, axis=0)
    m2 = pltpu.roll(jnp.where(lane >= LANES - 2, behind, row), 2, axis=1)
    m1 = pltpu.roll(jnp.where(lane >= LANES - 1, behind, row), 1, axis=1)
    p1 = pltpu.roll(jnp.where(lane < 1, ahead, row), LANES - 1, axis=1)
    p2 = pltpu.roll(jnp.where(lane < 2, ahead, row), LANES - 2, axis=1)
    return m2, m1, p1, p2


def along(centre, v_p, lane):
    m2, m1, p1, p2 = around(centre, lane)
    curve = ((m1 + p1) * 16.0 - (m2 + p2) - centre * 60.0) * SCALE
    return curve - v_p * ((p1 - m1) * 8.0 - (p2 - m2))


def across(field, r, v_r):
    weights = (-SCALE - v_r, 16.0 * SCALE + 8.0 * v_r, 16.0 * SCALE - 8.0 * v_r, v_r - SCALE)
    rows = (r - 2, r - 1, r + 1, r + 2)
    return sum(weight * field[row] for weight, row in zip(weights, rows) if row in field)


def tendency(field, r, v_r, v_p, lane):
    centre = field[r]
    m2, m1, p1, p2 = around(centre, lane)
    r_m2, r_m1, r_p1, r_p2 = field[r - 2], field[r - 1], field[r + 1], field[r + 2]
    near = (m1 + p1) + (r_m1 + r_p1)
    far = (m2 + p2) + (r_m2 + r_p2)
    slope_p = (p1 - m1) * 8.0 - (p2 - m2)
    slope_r = (r_p1 - r_m1) * 8.0 - (r_p2 - r_m2)
    curve = (near * 16.0 - far - centre * 60.0) * SCALE
    return curve - v_p * slope_p - v_r * slope_r


def row_of(arrived, part, r):
    blocks = arrived.shape[0] // (3 * ROWS)
    return arrived[pl.ds(part * ROWS + r, blocks, stride=3 * ROWS), :]


def send_kernel(fields, velocity, offsets, sent, noted):
    slabs = fields.shape[0] // ROWS
    blocks = sent.shape[0] // (3 * ROWS)
    speed = velocity[...] * (1.0 / 12.0)
    for k in range(blocks):
        at = k * 3 * ROWS
        if k < slabs:
            sent[pl.ds(at, ROWS), :] = fields[pl.ds(k * ROWS, ROWS), :]
        else:
            sent[pl.ds(at, ROWS), :] = jnp.zeros((ROWS, LANES), jnp.float32)
        sent[pl.ds(at + ROWS, 2 * ROWS), :] = speed
    noted[...] = jnp.zeros((ROWS, LANES), jnp.float32)
    noted[:1, :ROWS] = offsets[...].astype(jnp.float32)


def show_kernel(noted, arrived, to_chip, to_cross, kept):
    blocks = arrived.shape[0] // (3 * ROWS)
    lane = lax.broadcasted_iota(jnp.int32, (blocks, LANES), 1)
    first = lax.axis_index("rad") % 2 == 0
    slab = {r: row_of(arrived, 0, r) for r in range(ROWS)}
    v_r = {r: row_of(arrived, 1, r) for r in range(ROWS)}
    v_p = {r: row_of(arrived, 2, r) for r in range(ROWS)}

    def change(field, r):
        if 2 <= r < ROWS - 2:
            return tendency(field, r, v_r[r], v_p[r], lane)
        return along(field[r], v_p[r], lane) + across(field, r, v_r[r])

    alone = {r: slab[r] + change(slab, r) for r in range(ROWS)}
    for k in range(ROWS - 4):
        kept[pl.ds(k * blocks, blocks), :] = alone[2 + k]
    moved = {r: 0.5 * (slab[r] + alone[r] + change(alone, r)) for r in range(ROWS)}
    at = 0
    for count, rows in zip(SHOWN, (slab, alone, moved, v_r, v_p)):
        for k in range(count):
            near_low, near_high = rows[k], rows[ROWS - count + k]
            to_chip[pl.ds(at, blocks), :] = jnp.where(first, near_high, near_low)
            to_cross[pl.ds(at, blocks), :] = jnp.where(first, near_low, near_high)
            at += blocks
    for ref in (to_chip, to_cross):
        ref[pl.ds(at, ROWS), :] = noted[...]


def steps_kernel(
    arrived, kept, shown, chip, cross, out, state, section, ring, v_r, v_p, shifts, sem
):
    size = shown.shape[0]
    blocks = arrived.shape[0] // (3 * ROWS)
    lane = lax.broadcasted_iota(jnp.int32, (blocks, LANES), 1)
    place = lax.axis_index("rad")
    first = place % 2 == 0
    chip_at = (1 - place % 2) * size
    tails = [
        pltpu.make_async_copy(ref.at[pl.ds(at + size - ROWS, ROWS)], shifts.at[i], sem.at[i])
        for i, (ref, at) in enumerate(((shown, 0), (chip, chip_at), (cross, 0)))
    ]
    for tail in tails:
        tail.start()
    has_low = place > 0
    has_high = place < lax.axis_size("rad") - 1

    def inside(r, value):
        if r < ROWS:
            return jnp.where(has_low, value, 0.0)
        if r >= 2 * ROWS:
            return jnp.where(has_high, value, 0.0)
        return value

    for r in range(ROWS):
        state[ROWS + r] = row_of(arrived, 0, r)
        v_r[ROWS + r] = row_of(arrived, 1, r)
        v_p[ROWS + r] = row_of(arrived, 2, r)
    for k in range(ROWS - 4):
        section[ROWS + 2 + k] = kept[pl.ds(k * blocks, blocks), :]
    alone, moved = {}, {}
    at = 0
    for count, rows in zip(SHOWN, (state, alone, moved, v_r, v_p)):
        for k in range(count):
            from_chip = chip[pl.ds(chip_at + at, blocks), :]
            from_cross = cross[pl.ds(at, blocks), :]
            low, high = ROWS - count + k, 2 * ROWS + k
            rows[low] = inside(low, jnp.where(first, from_cross, from_chip))
            rows[high] = inside(high, jnp.where(first, from_chip, from_cross))
            at += blocks

    own = {r: state[r] for r in (8, 9, 14, 15)}
    bring = {r: inside(r, across(own, r, v_r[r])) for r in (6, 7, 16, 17)}
    for r in bring:
        section[r] = alone[r] + bring[r]
    for r in (8, 9, 14, 15):
        section[r] = state[r] + tendency(state, r, v_r[r], v_p[r], lane)

    def shift_of(r):
        local = r % ROWS
        if r // ROWS == 1:
            return shifts[0, 0, local].astype(jnp.int32)
        from_chip = shifts[1, 0, local]
        from_cross = shifts[2, 0, local]
        if r < ROWS:
            return jnp.where(first, from_cross, from_chip).astype(jnp.int32)
        return jnp.where(first, from_chip, from_cross).astype(jnp.int32)

    def shifted(r):
        offset = shift_of(r)
        hops = offset // LANES
        rest = offset % LANES
        near = ring[r, pl.ds(blocks - hops, blocks), :]
        far = ring[r, pl.ds(blocks - 1 - hops, blocks), :]
        return pltpu.roll(jnp.where(lane < LANES - rest, near, far), rest, axis=1)

    def renew(r, value):
        ring[r, :blocks, :] = value
        ring[r, blocks:, :] = value

    def heun(r):
        return 0.5 * (state[r] + section[r] + tendency(section, r, v_r[r], v_p[r], lane))

    for r in range(ROWS, 2 * ROWS):
        renew(r, heun(r))
    bring.update({r: section[r] for r in (8, 9, 14, 15)})
    for r in (4, 5, 6, 7, 16, 17, 18, 19):
        gain = across(bring, r, v_r[r])
        if r in bring:
            gain = gain + bring[r] + along(bring[r], v_p[r], lane)
        renew(r, inside(r, moved[r] + 0.5 * gain))
    for tail in tails:
        tail.wait()
    for r in range(4, 20):
        state[r] = shifted(r)
    for r in range(6, 18):
        section[r] = inside(r, state[r] + tendency(state, r, v_r[r], v_p[r], lane))
    for r in range(ROWS, 2 * ROWS):
        renew(r, heun(r))
    for r in range(ROWS, 2 * ROWS):
        out[pl.ds(r - ROWS, blocks, stride=ROWS), :] = shifted(r)


def in_vmem(value):
    return pltpu.with_memory_space_constraint(value, pltpu.VMEM)


def shards(fields, velocity, offsets):
    slabs = fields.shape[0] * fields.shape[1]
    blocks = lax.axis_size("az")
    count = lax.axis_size("rad")
    vmem = pl.BlockSpec(memory_space=pltpu.VMEM)

    sent, noted = pl.pallas_call(
        send_kernel,
        out_shape=[
            pltpu.VMEM((blocks * 3 * ROWS, LANES), jnp.float32),
            pltpu.VMEM((ROWS, LANES), jnp.float32),
        ],
        in_specs=[vmem] * 3,
        out_specs=[vmem] * 2,
        name="send",
    )(
        fields.reshape(slabs * ROWS, LANES),
        velocity.reshape(2 * ROWS, LANES),
        offsets.reshape(1, ROWS),
    )
    arrived = lax.all_to_all(sent.reshape(blocks, 3 * ROWS, LANES), "az", 0, 0, tiled=True)
    arrived = in_vmem(arrived.reshape(blocks * 3 * ROWS, LANES))
    size = sum(SHOWN) * blocks + ROWS
    to_chip, to_cross, kept = pl.pallas_call(
        show_kernel,
        out_shape=[pltpu.VMEM((rows, LANES), jnp.float32) for rows in (size, size, (ROWS - 4) * blocks)],
        in_specs=[vmem] * 2,
        out_specs=[vmem] * 3,
        name="show",
    )(in_vmem(noted), arrived)

    def device(a, r):
        return a * count + r % count

    swaps = [(device(a, r), device(a, r + 1)) for a in range(slabs) for r in range(1, count - 1, 2)]
    swaps += [(high, low) for low, high in swaps]
    twins = [[r, r + 1] for r in range(0, count, 2)]
    chip = lax.all_gather(to_chip, "rad", axis_index_groups=twins, tiled=True)
    cross = lax.ppermute(to_cross, ("az", "rad"), swaps)

    done = pl.pallas_call(
        steps_kernel,
        out_shape=pltpu.VMEM((blocks * ROWS, LANES), jnp.float32),
        in_specs=[vmem] * 5,
        out_specs=vmem,
        scratch_shapes=[
            pltpu.VMEM((3 * ROWS, blocks, LANES), jnp.float32),
            pltpu.VMEM((3 * ROWS, blocks, LANES), jnp.float32),
            pltpu.VMEM((3 * ROWS, 2 * blocks, LANES), jnp.float32),
            pltpu.VMEM((3 * ROWS, blocks, LANES), jnp.float32),
            pltpu.VMEM((3 * ROWS, blocks, LANES), jnp.float32),
            pltpu.SMEM((3, ROWS, LANES), jnp.float32),
            pltpu.SemaphoreType.DMA((3,)),
        ],
        name="disc_steps",
    )(arrived, in_vmem(kept), in_vmem(to_cross), in_vmem(chip), in_vmem(cross))
    back = lax.all_to_all(done.reshape(blocks, ROWS, LANES), "az", 0, 0, tiled=True)
    return back[:slabs].reshape(fields.shape)


def solution(mesh):
    placed = (P(None, None, "rad", "az"), P(None, "rad", "az"), P("rad"))
    return jax.shard_map(
        shards, mesh=mesh, in_specs=placed, out_specs=P(None, None, "rad", "az"), check_vma=False
    )
```

time: 49.3 us -> 48.8 us (0.990)
  waiting for transfers between devices: 3.3 us -> 2.8 us
    ppermute x1, waiting for transfers between devices: 3.3 us -> 2.8 us  [shards(): cross = lax.ppermute(to_cross, ('az', 'rad'), swaps)]
where the time goes in v6:
time: 48.8 us; the launch traced here: 48.6 us
  blocking collectives  30.3 us (62%)
  starting transfers between devices  12.5 us (26%)
  waiting for transfers between devices  2.8 us (6%)
  Pallas kernels  2.33 us (5%)
  local copies, waits for them, and re-layouts  0.62 us (1%)
    all_to_all x1, blocking collectives, shards(): lax.all_to_all(sent.reshape(blocks, 3 * ROWS, LANES), 'az', 0, 0, tiled=T...  18.5 us
    ppermute x1, starting transfers between devices, shards(): cross = lax.ppermute(to_cross, ('az', 'rad'), swaps)  12.5 us
    all_to_all x1, blocking collectives, shards(): lax.all_to_all(done.reshape(blocks, ROWS, LANES), 'az', 0, 0, tiled=True)  9.83 us
    ppermute x1, waiting for transfers between devices, shards(): cross = lax.ppermute(to_cross, ('az', 'rad'), swaps)  2.8 us
    all_gather x1, blocking collectives, shards(): chip = lax.all_gather(to_chip, 'rad', axis_index_groups=twins, tiled=True)  1.98 us
    pallas_call x1, Pallas kernels, shards(): pl.pallas_call(steps_kernel, out_shape=pltpu.VMEM((blocks * ROWS, LANES),...  1.28 us
  transfers between devices with their start and end apart: 1, of which 1 were waited for; matrix products, arithmetic and copies ran while one was open for 0% of the time, Pallas kernels for 0%

profile of v6, /device:TPU:1, one launch (start us, length us, event | category | flops | bytes accessed | tf_op | source)
XLA Modules:
  0.0 48.6 jit_solution(14775839611356144282)
XLA Ops:
  0.0 0.8 %send.1 = (f32[384,128]{1,0:T(8,128)S(1)}, f32[8,128]{1,0:T(8,128)S(1)}) custom-call(f32[80,128]{1,0:T(8,128)} %bitcast.11, f32[16,128]{1,0:T(8,128)} %bitcast.12, s32[1,8]{1,0:T(1,128)} %bitcast.13), custom_call_target="tpu_custom_call" | custom-call | tf_op jit(solution)/shard_map/send/pallas_call | solution.py:202
  0.8 18.5 %all_to_all.10 = f32[16,24,128]{2,1,0:T(8,128)S(1)} all-to-all(f32[16,24,128]{2,1,0:T(8,128)S(1)} %bitcast.10), channel_id=1, replica_groups=mesh['az'=16,'rad'=48] {'az'}, dimensions={0} | all-to-all | bytes 393216 | tf_op jit(solution)/shard_map/all_to_all | solution.py:216
  19.3 0.2 show.1
  19.6 12.5 %collective-permute-start = (f32[232,128]{1,0:T(8,128)S(1)}, f32[232,128]{1,0:T(8,128)S(1)}, u32[]{:S(2)}, u32[]{:S(2)}) collective-permute-start(f32[232,128]{1,0:T(8,128)S(1)} %get-tuple-element.13.shown), channel_id=1, source_target_pairs={{1,2},{3,4},{5,6},{7,8},{9,10},{11,12},{13,14},{15,16},{17,18},{19... | collective-permute-start | bytes 356360 | tf_op jit(solution)/shard_map/ppermute | solution.py:234
  32.0 2.0 %all_gather.3.chip = f32[464,128]{1,0:T(8,128)S(1)} all-gather(f32[232,128]{1,0:T(8,128)S(1)} %get-tuple-element.14), channel_id=1, replica_groups={{0,1},{2,3},{4,5},{6,7},{8,9},{10,11},{12,13},{14,15},{16,17},{18,19},{..., dimensions={0}, use_global_device_ids=true | all-gather | bytes 356352 | tf_op jit(solution)/shard_map/all_gather | solution.py:233
  34.0 2.8 %collective-permute-done.cross = f32[232,128]{1,0:T(8,128)S(1)} collective-permute-done((f32[232,128]{1,0:T(8,128)S(1)}, f32[232,128]{1,0:T(8,128)S(1)}, u32[]{:S(2)}, u32[]{:S(2)}) %collective-permute-start) | collective-permute-done | bytes 118816 | tf_op jit(solution)/shard_map/ppermute | solution.py:234
  36.8 1.3 %disc_steps.1 = f32[128,128]{1,0:T(8,128)S(1)} custom-call(f32[384,128]{1,0:T(8,128)S(1)} %bitcast.8, f32[64,128]{1,0:T(8,128)S(1)} %get-tuple-element.12.kept, f32[232,128]{1,0:T(8,128)S(1)} %get-tuple-element.13.shown, f32[464,128]{1,0:T(8,128)S(1)} %all_gather.3.chip, f32[232,128]{1,0:T(8,128)S(1)} %collective-permute-done.cross), custom_call_target="tpu_custom_call" | custom-call | tf_op jit(solution)/shard_map/disc_steps/pallas_call | solution.py:236
  38.1 9.8 %all_to_all.11 = f32[16,8,128]{2,1,0:T(8,128)S(1)} all-to-all(f32[16,8,128]{2,1,0:T(8,128)S(1)} %bitcast.9), channel_id=1, replica_groups=mesh['az'=16,'rad'=48] {'az'}, dimensions={0} | all-to-all | bytes 131072 | tf_op jit(solution)/shard_map/all_to_all | solution.py:252
  47.9 0.6 %slice.4 = f32[10,8,128]{2,1,0:T(8,128)} slice(f32[16,8,128]{2,1,0:T(8,128)S(1)} %all_to_all.11), slice={[0:10], [0:8], [0:128]} | slice | bytes 81920 | tf_op jit(solution)/shard_map/slice | solution.py:253
Async XLA Ops:
  19.6 17.3 %collective-permute-start = (f32[232,128]{1,0:T(8,128)S(1)}, f32[232,128]{1,0:T(8,128)S(1)}, u32[]{:S(2)}, u32[]{:S(2)}) collective-permute-start(f32[232,128]{1,0:T(8,128)S(1)} %get-tuple-element.13.shown), channel_id=1, source_target_pairs={{1,2},{3,4},{5,6},{7,8},{9,10},{11,12},{13,14},{15,16},{17,18},{19... | collective-permute-start | bytes 356360 | tf_op jit(solution)/shard_map/ppermute | solution.py:234

commit v7 on v6

--- a/solution.py
+++ b/solution.py
@@ -95,21 +95,13 @@
         ref[pl.ds(at, ROWS), :] = noted[...]
 
 
-def steps_kernel(
-    arrived, kept, shown, chip, cross, out, state, section, ring, v_r, v_p, shifts, sem
-):
+def steps_kernel(arrived, kept, shown, chip, cross, out, state, section, ring, v_r, v_p):
     size = shown.shape[0]
     blocks = arrived.shape[0] // (3 * ROWS)
     lane = lax.broadcasted_iota(jnp.int32, (blocks, LANES), 1)
     place = lax.axis_index("rad")
     first = place % 2 == 0
     chip_at = (1 - place % 2) * size
-    tails = [
-        pltpu.make_async_copy(ref.at[pl.ds(at + size - ROWS, ROWS)], shifts.at[i], sem.at[i])
-        for i, (ref, at) in enumerate(((shown, 0), (chip, chip_at), (cross, 0)))
-    ]
-    for tail in tails:
-        tail.start()
     has_low = place > 0
     has_high = place < lax.axis_size("rad") - 1
 
@@ -144,20 +136,22 @@
     for r in (8, 9, 14, 15):
         section[r] = state[r] + tendency(state, r, v_r[r], v_p[r], lane)
 
-    def shift_of(r):
-        local = r % ROWS
-        if r // ROWS == 1:
-            return shifts[0, 0, local].astype(jnp.int32)
-        from_chip = shifts[1, 0, local]
-        from_cross = shifts[2, 0, local]
-        if r < ROWS:
-            return jnp.where(first, from_cross, from_chip).astype(jnp.int32)
-        return jnp.where(first, from_chip, from_cross).astype(jnp.int32)
+    tail = pl.ds(size - ROWS, 1)
+    from_chip, from_cross = chip[pl.ds(chip_at + size - ROWS, 1), :], cross[tail, :]
+    noted = (
+        jnp.where(first, from_cross, from_chip),
+        shown[tail, :],
+        jnp.where(first, from_chip, from_cross),
+    )
+    cell = lax.broadcasted_iota(jnp.int32, (1, LANES), 1)
+    offsets = {
+        r: jnp.sum(jnp.where(cell == r % ROWS, noted[r // ROWS], 0.0)).astype(jnp.int32)
+        for r in range(4, 20)
+    }
 
     def shifted(r):
-        offset = shift_of(r)
-        hops = offset // LANES
-        rest = offset % LANES
+        hops = offsets[r] // LANES
+        rest = offsets[r] % LANES
         near = ring[r, pl.ds(blocks - hops, blocks), :]
         far = ring[r, pl.ds(blocks - 1 - hops, blocks), :]
         return pltpu.roll(jnp.where(lane < LANES - rest, near, far), rest, axis=1)
@@ -177,8 +171,6 @@
         if r in bring:
             gain = gain + bring[r] + along(bring[r], v_p[r], lane)
         renew(r, inside(r, moved[r] + 0.5 * gain))
-    for tail in tails:
-        tail.wait()
     for r in range(4, 20):
         state[r] = shifted(r)
     for r in range(6, 18):
@@ -244,8 +236,6 @@
             pltpu.VMEM((3 * ROWS, 2 * blocks, LANES), jnp.float32),
             pltpu.VMEM((3 * ROWS, blocks, LANES), jnp.float32),
             pltpu.VMEM((3 * ROWS, blocks, LANES), jnp.float32),
-            pltpu.SMEM((3, ROWS, LANES), jnp.float32),
-            pltpu.SemaphoreType.DMA((3,)),
         ],
         name="disc_steps",
     )(arrived, in_vmem(kept), in_vmem(to_cross), in_vmem(chip), in_vmem(cross))

time: 48.8 us -> 48.2 us (0.988)
  Pallas kernels: 2.33 us -> 1.76 us
    pallas_call x1, Pallas kernels: 1.28 us -> 0.71 us  [shards(): pl.pallas_call(steps_kernel, out_shape=pltpu.VMEM((blocks * ROWS, LANES),...]
where the time goes in v7:
time: 48.2 us; the launch traced here: 48 us
  blocking collectives  30.3 us (63%)
  starting transfers between devices  12.5 us (26%)
  waiting for transfers between devices  2.8 us (6%)
  Pallas kernels  1.76 us (4%)
  local copies, waits for them, and re-layouts  0.62 us (1%)
    all_to_all x1, blocking collectives, shards(): lax.all_to_all(sent.reshape(blocks, 3 * ROWS, LANES), 'az', 0, 0, tiled=T...  18.5 us
    ppermute x1, starting transfers between devices, shards(): cross = lax.ppermute(to_cross, ('az', 'rad'), swaps)  12.5 us
    all_to_all x1, blocking collectives, shards(): lax.all_to_all(done.reshape(blocks, ROWS, LANES), 'az', 0, 0, tiled=True)  9.83 us
    ppermute x1, waiting for transfers between devices, shards(): cross = lax.ppermute(to_cross, ('az', 'rad'), swaps)  2.8 us
    all_gather x1, blocking collectives, shards(): chip = lax.all_gather(to_chip, 'rad', axis_index_groups=twins, tiled=True)  1.98 us
  transfers between devices with their start and end apart: 1, of which 1 were waited for; matrix products, arithmetic and copies ran while one was open for 0% of the time, Pallas kernels for 0%

profile of v7, /device:TPU:1, one launch (start us, length us, event | category | flops | bytes accessed | tf_op | source)
XLA Modules:
  0.0 48.0 jit_solution(1999012483704083586)
XLA Ops:
  0.0 0.8 %send.1 = (f32[384,128]{1,0:T(8,128)S(1)}, f32[8,128]{1,0:T(8,128)S(1)}) custom-call(f32[80,128]{1,0:T(8,128)} %bitcast.11, f32[16,128]{1,0:T(8,128)} %bitcast.12, s32[1,8]{1,0:T(1,128)} %bitcast.13), custom_call_target="tpu_custom_call" | custom-call | tf_op jit(solution)/shard_map/send/pallas_call | solution.py:194
  0.8 18.5 %all_to_all.10 = f32[16,24,128]{2,1,0:T(8,128)S(1)} all-to-all(f32[16,24,128]{2,1,0:T(8,128)S(1)} %bitcast.10), channel_id=1, replica_groups=mesh['az'=16,'rad'=48] {'az'}, dimensions={0} | all-to-all | bytes 393216 | tf_op jit(solution)/shard_map/all_to_all | solution.py:208
  19.3 0.2 show.1
  19.6 12.5 %collective-permute-start = (f32[232,128]{1,0:T(8,128)S(1)}, f32[232,128]{1,0:T(8,128)S(1)}, u32[]{:S(2)}, u32[]{:S(2)}) collective-permute-start(f32[232,128]{1,0:T(8,128)S(1)} %get-tuple-element.13.shown), channel_id=1, source_target_pairs={{1,2},{3,4},{5,6},{7,8},{9,10},{11,12},{13,14},{15,16},{17,18},{19... | collective-permute-start | bytes 356360 | tf_op jit(solution)/shard_map/ppermute | solution.py:226
  32.0 2.0 %all_gather.3.chip = f32[464,128]{1,0:T(8,128)S(1)} all-gather(f32[232,128]{1,0:T(8,128)S(1)} %get-tuple-element.14), channel_id=1, replica_groups={{0,1},{2,3},{4,5},{6,7},{8,9},{10,11},{12,13},{14,15},{16,17},{18,19},{..., dimensions={0}, use_global_device_ids=true | all-gather | bytes 356352 | tf_op jit(solution)/shard_map/all_gather | solution.py:225
  34.0 2.8 %collective-permute-done.cross = f32[232,128]{1,0:T(8,128)S(1)} collective-permute-done((f32[232,128]{1,0:T(8,128)S(1)}, f32[232,128]{1,0:T(8,128)S(1)}, u32[]{:S(2)}, u32[]{:S(2)}) %collective-permute-start) | collective-permute-done | bytes 118816 | tf_op jit(solution)/shard_map/ppermute | solution.py:226
  36.8 0.7 %disc_steps.1 = f32[128,128]{1,0:T(8,128)S(1)} custom-call(f32[384,128]{1,0:T(8,128)S(1)} %bitcast.8, f32[64,128]{1,0:T(8,128)S(1)} %get-tuple-element.12.kept, f32[232,128]{1,0:T(8,128)S(1)} %get-tuple-element.13.shown, f32[464,128]{1,0:T(8,128)S(1)} %all_gather.3.chip, f32[232,128]{1,0:T(8,128)S(1)} %collective-permute-done.cross), custom_call_target="tpu_custom_call" | custom-call | tf_op jit(solution)/shard_map/disc_steps/pallas_call | solution.py:228
  37.5 9.8 %all_to_all.11 = f32[16,8,128]{2,1,0:T(8,128)S(1)} all-to-all(f32[16,8,128]{2,1,0:T(8,128)S(1)} %bitcast.9), channel_id=1, replica_groups=mesh['az'=16,'rad'=48] {'az'}, dimensions={0} | all-to-all | bytes 131072 | tf_op jit(solution)/shard_map/all_to_all | solution.py:242
  47.4 0.6 %slice.4 = f32[10,8,128]{2,1,0:T(8,128)} slice(f32[16,8,128]{2,1,0:T(8,128)S(1)} %all_to_all.11), slice={[0:10], [0:8], [0:128]} | slice | bytes 81920 | tf_op jit(solution)/shard_map/slice | solution.py:243
Async XLA Ops:
  19.6 17.3 %collective-permute-start = (f32[232,128]{1,0:T(8,128)S(1)}, f32[232,128]{1,0:T(8,128)S(1)}, u32[]{:S(2)}, u32[]{:S(2)}) collective-permute-start(f32[232,128]{1,0:T(8,128)S(1)} %get-tuple-element.13.shown), channel_id=1, source_target_pairs={{1,2},{3,4},{5,6},{7,8},{9,10},{11,12},{13,14},{15,16},{17,18},{19... | collective-permute-start | bytes 356360 | tf_op jit(solution)/shard_map/ppermute | solution.py:226

commit v8 on v7

--- a/solution.py
+++ b/solution.py
@@ -81,9 +81,10 @@
         return along(field[r], v_p[r], lane) + across(field, r, v_r[r])
 
     alone = {r: slab[r] + change(slab, r) for r in range(ROWS)}
-    for k in range(ROWS - 4):
-        kept[pl.ds(k * blocks, blocks), :] = alone[2 + k]
     moved = {r: 0.5 * (slab[r] + alone[r] + change(alone, r)) for r in range(ROWS)}
+    for r in range(ROWS):
+        kept[pl.ds(r * blocks, blocks), :] = alone[r]
+        kept[pl.ds((ROWS + r) * blocks, blocks), :] = moved[r]
     at = 0
     for count, rows in zip(SHOWN, (slab, alone, moved, v_r, v_p)):
         for k in range(count):
@@ -112,15 +113,15 @@
             return jnp.where(has_high, value, 0.0)
         return value
 
+    begun, alone, moved = {}, {}, {}
     for r in range(ROWS):
-        state[ROWS + r] = row_of(arrived, 0, r)
+        begun[ROWS + r] = row_of(arrived, 0, r)
+        alone[ROWS + r] = kept[pl.ds(r * blocks, blocks), :]
+        moved[ROWS + r] = kept[pl.ds((ROWS + r) * blocks, blocks), :]
         v_r[ROWS + r] = row_of(arrived, 1, r)
         v_p[ROWS + r] = row_of(arrived, 2, r)
-    for k in range(ROWS - 4):
-        section[ROWS + 2 + k] = kept[pl.ds(k * blocks, blocks), :]
-    alone, moved = {}, {}
     at = 0
-    for count, rows in zip(SHOWN, (state, alone, moved, v_r, v_p)):
+    for count, rows in zip(SHOWN, (begun, alone, moved, v_r, v_p)):
         for k in range(count):
             from_chip = chip[pl.ds(chip_at + at, blocks), :]
             from_cross = cross[pl.ds(at, blocks), :]
@@ -128,13 +129,6 @@
             rows[low] = inside(low, jnp.where(first, from_cross, from_chip))
             rows[high] = inside(high, jnp.where(first, from_chip, from_cross))
             at += blocks
-
-    own = {r: state[r] for r in (8, 9, 14, 15)}
-    bring = {r: inside(r, across(own, r, v_r[r])) for r in (6, 7, 16, 17)}
-    for r in bring:
-        section[r] = alone[r] + bring[r]
-    for r in (8, 9, 14, 15):
-        section[r] = state[r] + tendency(state, r, v_r[r], v_p[r], lane)
 
     tail = pl.ds(size - ROWS, 1)
     from_chip, from_cross = chip[pl.ds(chip_at + size - ROWS, 1), :], cross[tail, :]
@@ -160,14 +154,14 @@
         ring[r, :blocks, :] = value
         ring[r, blocks:, :] = value
 
-    def heun(r):
-        return 0.5 * (state[r] + section[r] + tendency(section, r, v_r[r], v_p[r], lane))
-
-    for r in range(ROWS, 2 * ROWS):
-        renew(r, heun(r))
-    bring.update({r: section[r] for r in (8, 9, 14, 15)})
-    for r in (4, 5, 6, 7, 16, 17, 18, 19):
-        gain = across(bring, r, v_r[r])
+    edge = (6, 7, 8, 9, 14, 15, 16, 17)
+    bring = {}
+    for r in edge:
+        others = {k: begun[k] for k in edge if k // ROWS != r // ROWS}
+        bring[r] = inside(r, across(others, r, v_r[r]))
+    whole = {r: alone[r] + bring[r] for r in edge}
+    for r in range(4, 20):
+        gain = across({k: (bring if k // ROWS == r // ROWS else whole)[k] for k in edge}, r, v_r[r])
         if r in bring:
             gain = gain + bring[r] + along(bring[r], v_p[r], lane)
         renew(r, inside(r, moved[r] + 0.5 * gain))
@@ -176,7 +170,8 @@
     for r in range(6, 18):
         section[r] = inside(r, state[r] + tendency(state, r, v_r[r], v_p[r], lane))
     for r in range(ROWS, 2 * ROWS):
-        renew(r, heun(r))
+        change = tendency(section, r, v_r[r], v_p[r], lane)
+        renew(r, 0.5 * (state[r] + section[r] + change))
     for r in range(ROWS, 2 * ROWS):
         out[pl.ds(r - ROWS, blocks, stride=ROWS), :] = shifted(r)
 
@@ -210,7 +205,7 @@
     size = sum(SHOWN) * blocks + ROWS
     to_chip, to_cross, kept = pl.pallas_call(
         show_kernel,
-        out_shape=[pltpu.VMEM((rows, LANES), jnp.float32) for rows in (size, size, (ROWS - 4) * blocks)],
+        out_shape=[pltpu.VMEM((rows, LANES), jnp.float32) for rows in (size, size, 2 * ROWS * blocks)],
         in_specs=[vmem] * 2,
         out_specs=[vmem] * 3,
         name="show",

time: 48.2 us -> 48.2 us (level)
  no operation moved by 1% of the time
where the time goes in v8:
time: 48.2 us; the launch traced here: 47.9 us
  blocking collectives  30.3 us (63%)
  starting transfers between devices  12.5 us (26%)
  waiting for transfers between devices  2.8 us (6%)
  Pallas kernels  1.7 us (4%)
  local copies, waits for them, and re-layouts  0.62 us (1%)
    all_to_all x1, blocking collectives, shards(): lax.all_to_all(sent.reshape(blocks, 3 * ROWS, LANES), 'az', 0, 0, tiled=T...  18.5 us
    ppermute x1, starting transfers between devices, shards(): cross = lax.ppermute(to_cross, ('az', 'rad'), swaps)  12.5 us
    all_to_all x1, blocking collectives, shards(): lax.all_to_all(done.reshape(blocks, ROWS, LANES), 'az', 0, 0, tiled=True)  9.83 us
    ppermute x1, waiting for transfers between devices, shards(): cross = lax.ppermute(to_cross, ('az', 'rad'), swaps)  2.8 us
    all_gather x1, blocking collectives, shards(): chip = lax.all_gather(to_chip, 'rad', axis_index_groups=twins, tiled=True)  1.98 us
  transfers between devices with their start and end apart: 1, of which 1 were waited for; matrix products, arithmetic and copies ran while one was open for 0% of the time, Pallas kernels for 0%

profile of v8, /device:TPU:1, one launch (start us, length us, event | category | flops | bytes accessed | tf_op | source)
XLA Modules:
  0.0 47.9 jit_solution(17435404062232775456)
XLA Ops:
  0.0 0.8 %send.1 = (f32[384,128]{1,0:T(8,128)S(1)}, f32[8,128]{1,0:T(8,128)S(1)}) custom-call(f32[80,128]{1,0:T(8,128)} %bitcast.11, f32[16,128]{1,0:T(8,128)} %bitcast.12, s32[1,8]{1,0:T(1,128)} %bitcast.13), custom_call_target="tpu_custom_call" | custom-call | tf_op jit(solution)/shard_map/send/pallas_call | solution.py:189
  0.8 18.5 %all_to_all.10 = f32[16,24,128]{2,1,0:T(8,128)S(1)} all-to-all(f32[16,24,128]{2,1,0:T(8,128)S(1)} %bitcast.10), channel_id=1, replica_groups=mesh['az'=16,'rad'=48] {'az'}, dimensions={0} | all-to-all | bytes 393216 | tf_op jit(solution)/shard_map/all_to_all | solution.py:203
  19.3 0.2 show.1
  19.6 12.5 %collective-permute-start = (f32[232,128]{1,0:T(8,128)S(1)}, f32[232,128]{1,0:T(8,128)S(1)}, u32[]{:S(2)}, u32[]{:S(2)}) collective-permute-start(f32[232,128]{1,0:T(8,128)S(1)} %get-tuple-element.13.shown), channel_id=1, source_target_pairs={{1,2},{3,4},{5,6},{7,8},{9,10},{11,12},{13,14},{15,16},{17,18},{19... | collective-permute-start | bytes 356360 | tf_op jit(solution)/shard_map/ppermute | solution.py:221
  32.0 2.0 %all_gather.3.chip = f32[464,128]{1,0:T(8,128)S(1)} all-gather(f32[232,128]{1,0:T(8,128)S(1)} %get-tuple-element.14), channel_id=1, replica_groups={{0,1},{2,3},{4,5},{6,7},{8,9},{10,11},{12,13},{14,15},{16,17},{18,19},{..., dimensions={0}, use_global_device_ids=true | all-gather | bytes 356352 | tf_op jit(solution)/shard_map/all_gather | solution.py:220
  34.0 2.8 %collective-permute-done.cross = f32[232,128]{1,0:T(8,128)S(1)} collective-permute-done((f32[232,128]{1,0:T(8,128)S(1)}, f32[232,128]{1,0:T(8,128)S(1)}, u32[]{:S(2)}, u32[]{:S(2)}) %collective-permute-start) | collective-permute-done | bytes 118816 | tf_op jit(solution)/shard_map/ppermute | solution.py:221
  36.8 0.6 %disc_steps.1 = f32[128,128]{1,0:T(8,128)S(1)} custom-call(f32[384,128]{1,0:T(8,128)S(1)} %bitcast.8, f32[256,128]{1,0:T(8,128)S(1)} %get-tuple-element.12.kept, f32[232,128]{1,0:T(8,128)S(1)} %get-tuple-element.13.shown, f32[464,128]{1,0:T(8,128)S(1)} %all_gather.3.chip, f32[232,128]{1,0:T(8,128)S(1)} %collective-permute-done.cross), custom_call_target="tpu_custom_call" | custom-call | tf_op jit(solution)/shard_map/disc_steps/pallas_call | solution.py:223
  37.5 9.8 %all_to_all.11 = f32[16,8,128]{2,1,0:T(8,128)S(1)} all-to-all(f32[16,8,128]{2,1,0:T(8,128)S(1)} %bitcast.9), channel_id=1, replica_groups=mesh['az'=16,'rad'=48] {'az'}, dimensions={0} | all-to-all | bytes 131072 | tf_op jit(solution)/shard_map/all_to_all | solution.py:237
  47.3 0.6 %slice.4 = f32[10,8,128]{2,1,0:T(8,128)} slice(f32[16,8,128]{2,1,0:T(8,128)S(1)} %all_to_all.11), slice={[0:10], [0:8], [0:128]} | slice | bytes 81920 | tf_op jit(solution)/shard_map/slice | solution.py:238
Async XLA Ops:
  19.6 17.3 %collective-permute-start = (f32[232,128]{1,0:T(8,128)S(1)}, f32[232,128]{1,0:T(8,128)S(1)}, u32[]{:S(2)}, u32[]{:S(2)}) collective-permute-start(f32[232,128]{1,0:T(8,128)S(1)} %get-tuple-element.13.shown), channel_id=1, source_target_pairs={{1,2},{3,4},{5,6},{7,8},{9,10},{11,12},{13,14},{15,16},{17,18},{19... | collective-permute-start | bytes 356360 | tf_op jit(solution)/shard_map/ppermute | solution.py:221

commit v9 on v8

--- a/solution.py
+++ b/solution.py
@@ -4,6 +4,7 @@
 from jax.experimental import pallas as pl
 from jax.experimental.pallas import tpu as pltpu
 from jax.sharding import PartitionSpec as P
+
 
 VISCOSITY = 0.05
 SCALE = VISCOSITY / 12.0
@@ -102,7 +103,7 @@
     lane = lax.broadcasted_iota(jnp.int32, (blocks, LANES), 1)
     place = lax.axis_index("rad")
     first = place % 2 == 0
-    chip_at = (1 - place % 2) * size
+    chip_at = 0
     has_low = place > 0
     has_high = place < lax.axis_size("rad") - 1
 
@@ -216,9 +217,9 @@
 
     swaps = [(device(a, r), device(a, r + 1)) for a in range(slabs) for r in range(1, count - 1, 2)]
     swaps += [(high, low) for low, high in swaps]
-    twins = [[r, r + 1] for r in range(0, count, 2)]
-    chip = lax.all_gather(to_chip, "rad", axis_index_groups=twins, tiled=True)
+    twins = [(device(a, r), device(a, r ^ 1)) for a in range(slabs) for r in range(count)]
     cross = lax.ppermute(to_cross, ("az", "rad"), swaps)
+    chip = lax.ppermute(to_chip, ("az", "rad"), twins)
 
     done = pl.pallas_call(
         steps_kernel,

time: 48.2 us -> 52.4 us (1.087)
  the two profiles are of different devices: /device:TPU:1 before, /device:TPU:40 now
where the time goes in v9:
time: 52.4 us; the launch traced here: 52.1 us
  blocking collectives  30.2 us (58%)
  starting transfers between devices  14.7 us (28%)
  waiting for transfers between devices  4.88 us (9%)
  Pallas kernels  1.7 us (3%)
  local copies, waits for them, and re-layouts  0.62 us (1%)
    all_to_all x1, blocking collectives, shards(): lax.all_to_all(sent.reshape(blocks, 3 * ROWS, LANES), 'az', 0, 0, tiled=T...  19.3 us
    ppermute x1, starting transfers between devices, shards(): cross = lax.ppermute(to_cross, ('az', 'rad'), swaps)  12.7 us
    all_to_all x1, blocking collectives, shards(): lax.all_to_all(done.reshape(blocks, ROWS, LANES), 'az', 0, 0, tiled=True)  11 us
    ppermute x1, waiting for transfers between devices, shards(): cross = lax.ppermute(to_cross, ('az', 'rad'), swaps)  4.88 us
    ppermute x1, starting transfers between devices, shards(): chip = lax.ppermute(to_chip, ('az', 'rad'), twins)  1.92 us
  transfers between devices with their start and end apart: 2, of which 1 were waited for; matrix products, arithmetic and copies ran while one was open for 0% of the time, Pallas kernels for 0%

profile of v9, /device:TPU:40, one launch (start us, length us, event | category | flops | bytes accessed | tf_op | source)
XLA Modules:
  0.0 52.1 jit_solution(8897527883713435666)
XLA Ops:
  0.0 0.8 %send.1 = (f32[384,128]{1,0:T(8,128)S(1)}, f32[8,128]{1,0:T(8,128)S(1)}) custom-call(f32[80,128]{1,0:T(8,128)} %bitcast.11, f32[16,128]{1,0:T(8,128)} %bitcast.12, s32[1,8]{1,0:T(1,128)} %bitcast.13), custom_call_target="tpu_custom_call" | custom-call | tf_op jit(solution)/shard_map/send/pallas_call | solution.py:190
  0.8 19.3 %all_to_all.10 = f32[16,24,128]{2,1,0:T(8,128)S(1)} all-to-all(f32[16,24,128]{2,1,0:T(8,128)S(1)} %bitcast.10), channel_id=1, replica_groups=mesh['az'=16,'rad'=48] {'az'}, dimensions={0} | all-to-all | bytes 393216 | tf_op jit(solution)/shard_map/all_to_all | solution.py:204
  20.1 0.2 show.1
  20.3 1.9 %collective-permute-start = (f32[232,128]{1,0:T(8,128)S(1)}, f32[232,128]{1,0:T(8,128)S(1)}, u32[]{:S(2)}, u32[]{:S(2)}) collective-permute-start(f32[232,128]{1,0:T(8,128)S(1)} %get-tuple-element.14), channel_id=1, source_target_pairs={{0,1},{1,0},{2,3},{3,2},{4,5},{5,4},{6,7},{7,6},{8,9},{9,8},{10,11... | collective-permute-start | bytes 356360 | tf_op jit(solution)/shard_map/ppermute | solution.py:222
  22.2 12.7 %collective-permute-start.1 = (f32[232,128]{1,0:T(8,128)S(1)}, f32[232,128]{1,0:T(8,128)S(1)}, u32[]{:S(2)}, u32[]{:S(2)}) collective-permute-start(f32[232,128]{1,0:T(8,128)S(1)} %get-tuple-element.13.shown), channel_id=1, source_target_pairs={{1,2},{3,4},{5,6},{7,8},{9,10},{11,12},{13,14},{15,16},{17,18},{19... | collective-permute-start | bytes 356360 | tf_op jit(solution)/shard_map/ppermute | solution.py:221
  35.0 0.0 collective-permute-done.chip
  35.0 4.9 %collective-permute-done.1.cross = f32[232,128]{1,0:T(8,128)S(1)} collective-permute-done((f32[232,128]{1,0:T(8,128)S(1)}, f32[232,128]{1,0:T(8,128)S(1)}, u32[]{:S(2)}, u32[]{:S(2)}) %collective-permute-start.1) | collective-permute-done | bytes 118816 | tf_op jit(solution)/shard_map/ppermute | solution.py:221
  39.9 0.6 %disc_steps.1 = f32[128,128]{1,0:T(8,128)S(1)} custom-call(f32[384,128]{1,0:T(8,128)S(1)} %bitcast.8, f32[256,128]{1,0:T(8,128)S(1)} %get-tuple-element.12.kept, f32[232,128]{1,0:T(8,128)S(1)} %get-tuple-element.13.shown, f32[232,128]{1,0:T(8,128)S(1)} %collective-permute-done.chip, f32[232,128]{1,0:T(8,128)S(1)} %collective-permute-done.1.cross), custom_call_target="tpu_custom_call" | custom-call | tf_op jit(solution)/shard_map/disc_steps/pallas_call | solution.py:224
  40.5 11.0 %all_to_all.11 = f32[16,8,128]{2,1,0:T(8,128)S(1)} all-to-all(f32[16,8,128]{2,1,0:T(8,128)S(1)} %bitcast.9), channel_id=1, replica_groups=mesh['az'=16,'rad'=48] {'az'}, dimensions={0} | all-to-all | bytes 131072 | tf_op jit(solution)/shard_map/all_to_all | solution.py:238
  51.5 0.6 %slice.4 = f32[10,8,128]{2,1,0:T(8,128)} slice(f32[16,8,128]{2,1,0:T(8,128)S(1)} %all_to_all.11), slice={[0:10], [0:8], [0:128]} | slice | bytes 81920 | tf_op jit(solution)/shard_map/slice | solution.py:239
Async XLA Ops:
  20.3 14.7 %collective-permute-start = (f32[232,128]{1,0:T(8,128)S(1)}, f32[232,128]{1,0:T(8,128)S(1)}, u32[]{:S(2)}, u32[]{:S(2)}) collective-permute-start(f32[232,128]{1,0:T(8,128)S(1)} %get-tuple-element.14), channel_id=1, source_target_pairs={{0,1},{1,0},{2,3},{3,2},{4,5},{5,4},{6,7},{7,6},{8,9},{9,8},{10,11... | collective-permute-start | bytes 356360 | tf_op jit(solution)/shard_map/ppermute | solution.py:222
  22.2 17.6 %collective-permute-start.1 = (f32[232,128]{1,0:T(8,128)S(1)}, f32[232,128]{1,0:T(8,128)S(1)}, u32[]{:S(2)}, u32[]{:S(2)}) collective-permute-start(f32[232,128]{1,0:T(8,128)S(1)} %get-tuple-element.13.shown), channel_id=1, source_target_pairs={{1,2},{3,4},{5,6},{7,8},{9,10},{11,12},{13,14},{15,16},{17,18},{19... | collective-permute-start | bytes 356360 | tf_op jit(solution)/shard_map/ppermute | solution.py:221
